TPU v7x, 128 devices: a whole 4x4x4 slice. The times are simulated.
128 devices in a mesh: atom: 16 (over y, x), mode: 8 (over z, core).
Axes of the slice: x: 4, y: 4, z: 4, core: 2. Of those that a mesh axis runs over, the one named last changes fastest.
Arguments:
- eigvec: bfloat16 [3, 4096, 2048], P(None, 'atom', 'mode'), may hold values from -0.0546875 to 0.0546875
- force: float32 [3, 3, 16, 4096], P(None, None, None, 'atom'), may hold values from -12 to 12
- bond: float32 [3, 16, 4096], P(None, None, 'atom'), may hold values from -6 to 6
- nbr: int32 [16, 4096], P(None, 'atom'), may hold values from 0 to 4095, as said below
- band: int32 [2, 2048], P(None, 'mode'), may hold values from 0 to 2048, as said below
- freq: float32 [2048], P('mode'), may hold values from 0.5 to 4, as said below
Outputs:
- diffusivity: float32 [2048], P('mode')
- conductivity: float32 [2048], P('mode')
Inputs may be any that keep to these rules, and one draw needn't show every extreme that they name: `nbr`: each entry is an atom whose position in atom order differs from that of its own atom by 1 to 128, counted cyclically over the 4096 atoms; the distance 128 occurs in every draw. For every mode i: max(0, i - 128) <= band[0, i] <= i < band[1, i] <= min(2048, i + 129); both outer limits are reached at some mode. `freq`: strictly increasing along the modes.
All inputs are finite; a program needn't handle non-finite values.
Results may differ from a plain program's by a relative error of at most 0.00057.
Values may be sent and summed in bfloat16 or wider, within the bound.
A program may use at most 64 MiB of HBM per device.

v0:
```python
import math

import jax
import jax.numpy as jnp
from jax import lax
from jax.sharding import PartitionSpec as P

ATOM_DEV = 256
MODE_DEV = 256
RIM = 128
HALF = 128
BROAD = 128


def extended(shard, sides, width, wrap):
    for axis, dim in sides:
        size, length = (lax.axis_size(axis), shard.shape[dim])
        up = [(i, (i + 1) % size) for i in range(size if wrap else size - 1)]
        down = [(j, i) for i, j in up]
        last = lax.slice_in_dim(shard, length - width, length, axis=dim)
        first = lax.slice_in_dim(shard, 0, width, axis=dim)
        before = lax.ppermute(last, axis, up)
        after = lax.ppermute(first, axis, down)
        shard = jnp.concatenate([before, shard, after], axis=dim)
    return shard


def prefix(part, axis, combine, identity):
    place = lax.axis_index(axis)
    gathered = lax.all_gather(part, axis)
    state = jnp.zeros_like(part) + jnp.asarray(identity, part.dtype)

    def one(lap, state):
        return combine(state, lax.dynamic_index_in_dim(gathered, lap, 0, False))

    return lax.fori_loop(0, place, one, state)


def capacity_of(spectral):
    return spectral * spectral * jnp.exp(spectral) / jnp.expm1(spectral) ** 2


def pair_weight(own_freq, partner_freq, own_ids, partner_ids, lower_end, upper_end, broaden):
    inside = (
        (partner_ids[:, None] >= lower_end[None, :])
        & (partner_ids[:, None] < upper_end[None, :])
        & (partner_ids[:, None] != own_ids[None, :])
    )
    detune = own_freq[None, :] - partner_freq[:, None]
    lorentz = broaden / math.pi / (detune * detune + broaden * broaden)
    factor = (own_freq[None, :] + partner_freq[:, None]) ** 2 / (
        4.0 * own_freq[None, :] * partner_freq[:, None]
    )
    return jnp.where(inside, lorentz * factor, 0.0)


def add_totals(earlier, later):
    return earlier + later


def body(eigvec, force, bond, nbr, band, freq):
    atom_count = ATOM_DEV * lax.axis_size("atom")
    mode_count = MODE_DEV * lax.axis_size("mode")
    partner_span = MODE_DEV + 2 * HALF
    spectrum = lax.all_gather(freq, "mode", axis=0, tiled=True)
    atom_rows = extended(eigvec, (("atom", 1),), RIM, True)
    band_rows = extended(eigvec, (("mode", 2),), HALF, False)
    row_major = jnp.transpose(atom_rows, (1, 0, 2))
    domain = lax.axis_index("atom")
    local_ids = (nbr - domain * ATOM_DEV + RIM + atom_count) % atom_count
    block_size = min(512, ATOM_DEV)
    gathered = jnp.take(row_major, local_ids, axis=0)
    coupling = (bond[:, None, None, :, 0:block_size] * force[None, :, :, :, 0:block_size]).astype(
        jnp.bfloat16
    )
    block_image = jnp.einsum(
        "kcdna,nadi->kcai", coupling, gathered, preferred_element_type=jnp.float32
    )
    pieces = block_image.astype(jnp.bfloat16)
    pair_terms = jnp.einsum("caj,kcai->kji", band_rows, pieces, preferred_element_type=jnp.float32)
    mode_block = lax.axis_index("mode")
    mode_start = mode_block * MODE_DEV
    broaden = BROAD * (jnp.max(spectrum) - jnp.min(spectrum)) / (mode_count - 1)
    padded_freq = jnp.pad(spectrum, (HALF, HALF), constant_values=1.0)
    partner_freq = lax.dynamic_slice_in_dim(padded_freq, mode_start, partner_span)
    partner_ids = mode_start - HALF + jnp.arange(partner_span, dtype=jnp.int32)
    own_ids = mode_start + jnp.arange(MODE_DEV, dtype=jnp.int32)
    weight = pair_weight(freq, partner_freq, own_ids, partner_ids, band[0], band[1], broaden)
    summed_pair = lax.psum(pair_terms, "atom")
    strength = jnp.sum(summed_pair * summed_pair, axis=0)
    row_sums = jnp.sum(weight * strength, axis=0)
    diffusivity = math.pi / (3.0 * freq * freq) * row_sums
    running = jnp.cumsum(capacity_of(freq) * diffusivity)
    device_total = running[-1]
    earlier_sum = prefix(device_total, "mode", add_totals, jnp.float32(0.0))
    conductivity = (earlier_sum + running) / MODE_DEV
    return (diffusivity, conductivity)


def solution(mesh):
    in_specs = (
        P(None, "atom", "mode"),
        P(None, None, None, "atom"),
        P(None, None, "atom"),
        P(None, "atom"),
        P(None, "mode"),
        P("mode"),
    )
    out_specs = (P("mode"), P("mode"))
    return jax.shard_map(body, mesh=mesh, in_specs=in_specs, out_specs=out_specs, check_vma=False)
```

profile of v0, /device:TPU:97, one launch (start us, length us, event | category | flops | bytes accessed | tf_op | source)
XLA Modules:
  0.0 190.9 jit_solution(17926169755393144528)
XLA Ops:
  7.2 0.0 copy-start
  7.2 0.0 all-reduce.4.cloned.1.call-start
  7.2 1.4 copy.12
  8.6 0.0 copy-start.4
  8.6 0.2 fusion.21
  8.8 5.0 %collective-permute-start.1 = (bf16[3,128,256]{2,0,1:T(4,128)(2,1)S(1)}, bf16[3,128,256]{2,0,1:T(4,128)(2,1)}, u32[]{:S(2)}, u32[]{:S(2)}) collective-permute-start(bf16[3,128,256]{2,0,1:T(4,128)(2,1)S(1)} %get-tuple-element.39), channel_id=1, source_target_pairs={{8,0},{16,8},{24,16},{32,24},{40,32},{48,40},{56,48},{64,56},{72,6... | collective-permute-start | bytes 589832 | tf_op jit(solution)/shard_map/ppermute | solution.py:23
  13.8 0.0 collective-permute-start
  13.8 0.0 copy-done
  13.8 0.8 fusion.22
  14.7 3.5 %collective-permute-start.3 = (bf16[3,256,128]{2,1,0:T(8,128)(2,1)}, bf16[3,256,128]{2,1,0:T(8,128)(2,1)}, u32[]{:S(2)}, u32[]{:S(2)}) collective-permute-start(bf16[3,256,128]{2,1,0:T(8,128)(2,1)} %get-tuple-element.41), channel_id=1, source_target_pairs={{1,0},{2,1},{3,2},{4,3},{5,4},{6,5},{7,6},{9,8},{10,9},{11,10},{12... | collective-permute-start | bytes 589832 | tf_op jit(solution)/shard_map/ppermute | solution.py:23
  18.2 1.3 collective-permute-start.2
  19.6 0.7 copy.17
  20.3 1.1 copy.16
  21.4 0.7 copy.11
  22.1 0.0 collective-permute-done.1
  22.1 2.1 %collective-permute-done = bf16[3,128,256]{2,0,1:T(4,128)(2,1)} collective-permute-done((bf16[3,128,256]{2,0,1:T(4,128)(2,1)S(1)}, bf16[3,128,256]{2,0,1:T(4,128)(2,1)}, u32[]{:S(2)}, u32[]{:S(2)}) %collective-permute-start) | collective-permute-done | bytes 196640 | tf_op jit(solution)/shard_map/ppermute | solution.py:22
  24.2 1.8 maximum_bitcast_fusion
  25.9 32.8 %gather_fusion = bf16[4096,3,256]{2,1,0:T(4,128)(2,1)} fusion(bf16[512,3,256]{2,1,0:T(4,128)(2,1)S(1)} %maximum_bitcast_fusion, s32[4096]{0:T(1024)S(1)} %broadcast_clamp_fusion), kind=kCustom, calls=%fused_computation | custom fusion | bytes 12599296 | tf_op jit(solution)/shard_map/jit(_take)/gather | solution.py:72
  58.7 0.0 copy-done.1
  58.7 9.2 %fusion.8 = bf16[3,3,256,256]{3,1,0,2:T(4,128)(2,1)S(1)} fusion(f32[3,3,16,256]{2,0,1,3:T(4,128)S(1)} %copy.17, f32[3,16,256]{1,0,2:T(4,128)S(1)} %copy-done.1, bf16[16,256,3,256]{3,2,1,0:T(4,128)(2,1)} %bitcast.42, pred[16,256]{0,1:T(8,128)(4,1)} %copy.11), kind=kOutput, calls=%fused_computation.11 | convolution fusion | flops 60579840 | bytes 7671808 | tf_op jit(solution)/shard_map/kcdna,nadi->kcai/dot_general | solution.py:76
  68.0 0.0 collective-permute-done.3
  68.0 0.0 collective-permute-done.2
  68.0 3.0 %convolution_bitcast_fusion = f32[3,512,256]{1,2,0:T(8,128)} fusion(bf16[3,3,256,256]{3,1,0,2:T(4,128)(2,1)S(1)} %fusion.8, bf16[3,256,128]{2,1,0:T(8,128)(2,1)} %collective-permute-done.3, bf16[3,256,256]{2,1,0:T(8,128)(2,1)S(1)} %copy-done, bf16[3,256,128]{2,1,0:T(8,128)(2,1)} %collective-permute-done.2), kind=kOutput, calls=%fused_computation.12 | convolution fusion | flops 606339072 | bytes 3538944 | tf_op jit(solution)/shard_map/caj,kcai->kji/dot_general | solution.py:80
  71.0 0.0 all-reduce.4.cloned.1.call-update
  71.0 0.6 copy-done.5
  71.7 8.7 %all-gather = f32[8,1,256]{2,1,0:T(1,128)S(1)} all-gather(f32[1,1,256]{2,1,0:T(1,128)S(1)} %bitcast.45), channel_id=1, replica_groups=mesh['atom'=16,'mode'=8] {'mode'}, dimensions={0}, use_global_device_ids=true | all-gather | bytes 9216 | tf_op jit(solution)/shard_map/all_gather | solution.py:65
  80.4 0.6 fusion.20
  82.3 0.6 dynamic-slice
  82.9 0.1 pad_dynamic-slice_fusion
  83.0 74.8 %all-reduce.4.cloned.1.call-done = f32[3,512,256]{1,2,0:T(8,128)} async-done(((f32[3,512,256]{1,2,0:T(8,128)}), f32[3,512,256]{1,2,0:T(8,128)}) %all-reduce.4.cloned.1.call-update) | async-done | bytes 1572880 | tf_op jit(solution)/shard_map/psum | solution.py:89
  157.8 1.6 multiply_reduce_fusion
  159.5 0.5 multiply_reduce_fusion.1
  160.0 0.6 multiply_bitcast_fusion
  160.5 0.3 reduce-window.9
  160.9 0.1 slice.34
  161.0 0.1 slice_reduce_fusion
  161.1 0.1 add_bitcast_fusion
  161.2 0.8 slice_dynamic-update-slice_fusion
  161.9 11.9 %all-reduce.1 = f32[8]{0:T(128)S(1)} all-reduce(f32[8]{0:T(128)S(1)} %slice_dynamic-update-slice_fusion), channel_id=1, replica_groups=mesh['atom'=16,'mode'=8] {'mode'}, use_global_device_ids=true, to_apply=%add.1 | all-reduce | flops 8 | bytes 64
  173.8 9.7 %while.10 = (s32[]{:T(128)}, f32[]{:T(128)}, s32[]{:T(128)}, f32[8]{0:T(128)S(1)}, s32[]{:T(128)}, /*index=5*/s32[]{:T(128)}, s32[]{:T(128)}) while((s32[]{:T(128)}, f32[]{:T(128)}, s32[]{:T(128)}, f32[8]{0:T(128)S(1)}, s32[]{:T(128)}, /*index=5*/s32[]{:T(128)}, s32[]{:T(128)}) %tuple.27), condition=%wide.region_8.9_spmd, body=%wide.region_7.8_spmd.sunk | while | flops 6 | bytes 143 | solution.py:36
  173.8 0.7 dynamic_slice.10
  175.2 0.7 dynamic_slice.10
  176.6 0.7 dynamic_slice.10
  178.0 0.7 dynamic_slice.10
  179.3 0.7 dynamic_slice.10
  180.7 0.7 dynamic_slice.10
  182.1 0.7 dynamic_slice.10
  183.5 0.6 add_multiply_fusion
  (21 shorter events, 0.1 us)
Async XLA Ops:
  7.2 6.7 %copy-start = (bf16[3,256,256]{2,1,0:T(8,128)(2,1)S(1)}, bf16[3,256,256]{2,1,0:T(8,128)(2,1)}, u32[]{:S(2)}) copy-start(bf16[3,256,256]{2,1,0:T(8,128)(2,1)} %param.8) | copy-start | bytes 1179652
  7.2 12.3 %copy-start.3 = (s32[16,256]{1,0:T(8,128)S(1)}, s32[16,256]{1,0:T(8,128)}, u32[]{:S(2)}) copy-start(s32[16,256]{1,0:T(8,128)} %param.11) | copy-start | bytes 49156
  7.2 12.4 %copy-start.2 = (f32[3,3,16,256]{3,2,1,0:T(8,128)S(1)}, f32[3,3,16,256]{3,2,1,0:T(8,128)}, u32[]{:S(2)}) copy-start(f32[3,3,16,256]{3,2,1,0:T(8,128)} %param.9) | copy-start | bytes 442372
  7.2 150.6 %all-reduce.4.cloned.1.call-start = ((), (), s32[]{:S(2)}) async-start(), calls=%async_computation | async-start | bytes 3145728 | tf_op jit(solution)/shard_map/psum | solution.py:89
  8.6 11.7 %copy-start.4 = (f32[3,16,256]{2,1,0:T(8,128)S(1)}, f32[3,16,256]{2,1,0:T(8,128)}, u32[]{:S(2)}) copy-start(f32[3,16,256]{2,1,0:T(8,128)} %param.10) | copy-start | bytes 147460
  8.8 13.3 %collective-permute-start.1 = (bf16[3,128,256]{2,0,1:T(4,128)(2,1)S(1)}, bf16[3,128,256]{2,0,1:T(4,128)(2,1)}, u32[]{:S(2)}, u32[]{:S(2)}) collective-permute-start(bf16[3,128,256]{2,0,1:T(4,128)(2,1)S(1)} %get-tuple-element.39), channel_id=1, source_target_pairs={{8,0},{16,8},{24,16},{32,24},{40,32},{48,40},{56,48},{64,56},{72,6... | collective-permute-start | bytes 589832 | tf_op jit(solution)/shard_map/ppermute | solution.py:23
  13.8 10.3 %collective-permute-start = (bf16[3,128,256]{2,0,1:T(4,128)(2,1)S(1)}, bf16[3,128,256]{2,0,1:T(4,128)(2,1)}, u32[]{:S(2)}, u32[]{:S(2)}) collective-permute-start(bf16[3,128,256]{2,0,1:T(4,128)(2,1)S(1)} %get-tuple-element.38), channel_id=1, source_target_pairs={{0,8},{8,16},{16,24},{24,32},{32,40},{40,48},{48,56},{56,64},{64,7... | collective-permute-start | bytes 589832 | tf_op jit(solution)/shard_map/ppermute | solution.py:22
  14.7 53.3 %collective-permute-start.3 = (bf16[3,256,128]{2,1,0:T(8,128)(2,1)}, bf16[3,256,128]{2,1,0:T(8,128)(2,1)}, u32[]{:S(2)}, u32[]{:S(2)}) collective-permute-start(bf16[3,256,128]{2,1,0:T(8,128)(2,1)} %get-tuple-element.41), channel_id=1, source_target_pairs={{1,0},{2,1},{3,2},{4,3},{5,4},{6,5},{7,6},{9,8},{10,9},{11,10},{12... | collective-permute-start | bytes 589832 | tf_op jit(solution)/shard_map/ppermute | solution.py:23
  18.2 49.8 %collective-permute-start.2 = (bf16[3,256,128]{2,1,0:T(8,128)(2,1)}, bf16[3,256,128]{2,1,0:T(8,128)(2,1)}, u32[]{:S(2)}, u32[]{:S(2)}) collective-permute-start(bf16[3,256,128]{2,1,0:T(8,128)(2,1)} %get-tuple-element.40), channel_id=1, source_target_pairs={{0,1},{1,2},{2,3},{3,4},{4,5},{5,6},{6,7},{8,9},{9,10},{10,11},{11... | collective-permute-start | bytes 589832 | tf_op jit(solution)/shard_map/ppermute | solution.py:22
  25.9 32.8 %copy-start.1 = (f32[3,16,256]{1,0,2:T(4,128)S(1)}, f32[3,16,256]{1,0,2:T(4,128)}, u32[]{:S(2)}) copy-start(f32[3,16,256]{1,0,2:T(4,128)} %copy.16) | copy-start | bytes 147460
  71.0 0.7 copy-start.5
  71.0 11.3 %copy-start.7 = (u32[128]{0:T(128)S(1)}, u32[128]{0:T(128)}, u32[]{:S(2)}) copy-start(u32[128]{0:T(128)} %constant.93) | copy-start | bytes 1540
  71.0 12.0 %copy-start.6 = (s32[2,256]{1,0:T(2,128)S(1)}, s32[2,256]{1,0:T(2,128)}, u32[]{:S(2)}) copy-start(s32[2,256]{1,0:T(2,128)} %param.12) | copy-start | bytes 6148
Sparse Core Ops, SparseCore 0:
  71.1 86.6 all-reduce.3
where the time goes:
time: 191 us
  waiting for transfers between devices  76.9 us (40%)
  local copies, waits for them, and re-layouts  44.7 us (23%)
  blocking collectives  20.6 us (11%)
  between operations  15.5 us (8%)
  matrix products  12.2 us (6%)
  starting transfers between devices  9.86 us (5%)
  other arithmetic  6.15 us (3%)
  loops' own time  5 us (3%)
    psum x1, waiting for transfers between devices, body(): summed_pair = lax.psum(pair_terms, 'atom')  74.8 us
    gather x1, local copies, waits for them, and re-layouts, body(): gathered = jnp.take(row_major, local_ids, axis=0)  32.8 us
    unnamed x1, blocking collectives  11.9 us
    dot_general x1, matrix products, body(): jnp.einsum('kcdna,nadi->kcai', coupling, gathered, preferred_element_type...  9.23 us
    all_gather x1, blocking collectives, body(): spectrum = lax.all_gather(freq, 'mode', axis=0, tiled=True)  8.7 us
    ppermute x2, starting transfers between devices, extended(): after = lax.ppermute(first, axis, down)  8.54 us
    unnamed x23, local copies, waits for them, and re-layouts  5.23 us
    another operation x1, loops' own time, prefix(): return lax.fori_loop(0, place, one, state)  5 us
  transfers between devices with their start and end apart: 5, of which 2 were waited for; matrix products, arithmetic and copies ran while one was open for 25% of the time, Pallas kernels for 0%

commit v1 on v0

v1 whole, which is shorter than its diff:
```python
import functools
import math

import jax
import jax.numpy as jnp
from jax import lax
from jax.experimental import pallas as pl
from jax.experimental.pallas import tpu as pltpu
from jax.sharding import PartitionSpec as P

ATOM_DEV = 256
MODE_DEV = 256
NBR = 16
RIM = 128
HALF = 128
BROAD = 128
GROUP = 16
GROUPS = ATOM_DEV // GROUP
REACH = ATOM_DEV + RIM
ROWS = 8
BF16 = jnp.bfloat16
F32 = jnp.float32
MESH = pl.DeviceIdType.MESH


def iota(shape, dim):
    return lax.broadcasted_iota(jnp.int32, shape, dim)


def contract(lhs, rhs, lhs_dim, rhs_dim):
    return lax.dot_general(
        lhs, rhs, (((lhs_dim,), (rhs_dim,)), ((), ())), preferred_element_type=F32
    )


def kernel(
    n_atom,
    n_mode,
    eig_hbm,
    force_hbm,
    bond_hbm,
    nbr_hbm,
    band_hbm,
    freq_hbm,
    diff_ref,
    cond_ref,
    eig,
    force,
    bond,
    nbr,
    band,
    spectrum,
    low_rows,
    high_rows,
    low_cols,
    high_cols,
    nbr_rows,
    hot,
    spread,
    own_m,
    rim_m,
    flux,
    eig_t,
    send_pair,
    recv_pair,
    freq_col,
    send_sum,
    recv_sum,
    send_total,
    recv_total,
    local_sem,
    row_send,
    row_recv,
    col_send,
    col_recv,
    freq_send,
    freq_recv,
    pair_send,
    pair_recv,
    sum_send,
    sum_recv,
    total_send,
    total_recv,
):
    me = lax.axis_index("atom")
    block = lax.axis_index("mode")
    atoms = n_atom * ATOM_DEV

    barrier = pltpu.get_barrier_semaphore()

    def greet_atom(q, carry):
        pl.semaphore_signal(
            barrier, inc=1, device_id=(lax.rem(me + q, n_atom), block), device_id_type=MESH
        )
        return carry

    def greet_mode(q, carry):
        pl.semaphore_signal(
            barrier, inc=1, device_id=(me, lax.rem(block + q, n_mode)), device_id_type=MESH
        )
        return carry

    lax.fori_loop(1, n_atom, greet_atom, 0)
    lax.fori_loop(1, n_mode, greet_mode, 0)

    loads = [
        pltpu.make_async_copy(nbr_hbm, nbr, local_sem.at[0]),
        pltpu.make_async_copy(bond_hbm, bond, local_sem.at[1]),
        pltpu.make_async_copy(force_hbm, force, local_sem.at[2]),
        pltpu.make_async_copy(eig_hbm, eig, local_sem.at[3]),
        pltpu.make_async_copy(band_hbm, band, local_sem.at[4]),
        pltpu.make_async_copy(freq_hbm, spectrum.at[pl.ds(0, 1), :], local_sem.at[5]),
    ]
    for load in loads:
        load.start()

    lane = iota((ATOM_DEV, 256), 1)
    diagonal = (iota((ATOM_DEV, 256), 0) & (GROUP - 1)) == (lane & (GROUP - 1))
    slot_rows = jnp.where(
        (iota((NBR, 256), 1) >> 4) == iota((NBR, 256), 0), 1.0, 0.0
    ).astype(BF16)

    loads[0].wait()
    place = ((nbr[...] - me * ATOM_DEV + RIM + atoms) & (atoms - 1)) - RIM
    column = jnp.where(place < 0, place + REACH, place)
    coarse = contract((column >> 4).astype(F32).astype(BF16), slot_rows, 0, 0)
    fine = contract((column & 15).astype(F32).astype(BF16), slot_rows, 0, 0)
    column_of = jnp.where(diagonal, coarse * 16.0 + fine, 0.0)
    nbr_rows[...] = jnp.sum(column_of.reshape(GROUPS, GROUP, 256), axis=1)

    loads[5].wait()
    loads[3].wait()
    pl.semaphore_wait(barrier, n_atom + n_mode - 2)

    def to_atom(src, dst, q, send, recv):
        return pltpu.make_async_remote_copy(
            src_ref=src,
            dst_ref=dst,
            send_sem=send,
            recv_sem=recv,
            device_id=(lax.rem(me + q, n_atom), block),
            device_id_type=MESH,
        )

    def to_mode(src, dst, q, send, recv):
        return pltpu.make_async_remote_copy(
            src_ref=src,
            dst_ref=dst,
            send_sem=send,
            recv_sem=recv,
            device_id=(me, lax.rem(block + q, n_mode)),
            device_id_type=MESH,
        )

    up_rows = to_atom(
        eig.at[:, pl.ds(ATOM_DEV - RIM, RIM), :], low_rows, 1, row_send.at[0], row_recv.at[0]
    )
    down_rows = to_atom(
        eig.at[:, pl.ds(0, RIM), :], high_rows, n_atom - 1, row_send.at[1], row_recv.at[1]
    )
    up_cols = to_mode(
        eig.at[:, :, pl.ds(MODE_DEV - HALF, HALF)], low_cols, 1, col_send.at[0], col_recv.at[0]
    )
    down_cols = to_mode(
        eig.at[:, :, pl.ds(0, HALF)], high_cols, n_mode - 1, col_send.at[1], col_recv.at[1]
    )
    up_rows.start()
    down_rows.start()

    @pl.when(block < n_mode - 1)
    def _():
        up_cols.start()

    @pl.when(block > 0)
    def _():
        down_cols.start()

    def send_freq(q, carry):
        to_mode(
            spectrum.at[pl.ds(0, 1), :],
            spectrum.at[pl.ds(q, 1), :],
            q,
            freq_send,
            freq_recv,
        ).start()
        return carry

    lax.fori_loop(1, n_mode, send_freq, 0)

    reach_rows = iota((REACH, 256), 0).astype(F32)

    def one_hot(g, carry):
        hot[g] = jnp.where(reach_rows == nbr_rows[pl.ds(g, 1), :], 1.0, 0.0).astype(BF16)
        return carry

    lax.fori_loop(0, GROUPS, one_hot, 0)

    loads[1].wait()
    loads[2].wait()

    def build(k):
        for c in range(3):
            for d in range(3):
                coupling = (bond[k] * force[c, d]).astype(BF16)
                wide = jnp.where(diagonal, contract(coupling, slot_rows, 0, 0), 0.0).astype(BF16)
                first = (3 * c + d) * GROUP
                spread[:, first : first + GROUP, :] = wide.reshape(GROUPS, GROUP, 256)

        def group(g, carry):
            dense = contract(spread[g], hot[g], 1, 1).astype(BF16)
            for c in range(3):
                for d in range(3):
                    first = (3 * c + d) * GROUP
                    part = dense[first : first + GROUP]
                    rows = pl.ds(pl.multiple_of(g * GROUP, GROUP), GROUP)
                    own_m[c, rows, d * ATOM_DEV : (d + 1) * ATOM_DEV] = part[:, :ATOM_DEV]
                    rim_m[c, rows, d * RIM : (d + 1) * RIM] = part[:, ATOM_DEV:]
            return carry

        lax.fori_loop(0, GROUPS, group, 0)

    row = iota((HALF, HALF), 0)
    col = iota((HALF, HALF), 1)

    def project(k):
        inner = contract(
            own_m[...].reshape(3 * ATOM_DEV, 3 * ATOM_DEV),
            eig[...].reshape(3 * ATOM_DEV, MODE_DEV),
            1,
            0,
        ).reshape(3, ATOM_DEV, MODE_DEV)
        for h, halo in enumerate((low_rows, high_rows)):
            outer = contract(
                rim_m[:, h * RIM : (h + 1) * RIM, :].reshape(3 * RIM, 3 * RIM),
                halo[...].reshape(3 * RIM, MODE_DEV),
                1,
                0,
            ).reshape(3, RIM, MODE_DEV)
            flux[:, h * RIM : (h + 1) * RIM, :] = (
                inner[:, h * RIM : (h + 1) * RIM, :] + outer
            ).astype(BF16)
        pair = contract(eig_t[...], flux[...].reshape(3 * ATOM_DEV, MODE_DEV), 1, 0)
        for h in range(2):
            ours = slice(h * HALF, (h + 1) * HALF)
            before = pair[h * HALF : (h + 1) * HALF, ours]
            level = pair[(h + 1) * HALF : (h + 2) * HALF, ours]
            after = pair[(h + 2) * HALF : (h + 3) * HALF, ours]
            outer = jnp.where(row > col, before, after)
            inner_part = jnp.where(row == col, before, level)
            send_pair[k, :, 2 * h] = outer.reshape(n_atom, ROWS, HALF)
            send_pair[k, :, 2 * h + 1] = inner_part.reshape(n_atom, ROWS, HALF)

        def send(q, carry):
            to_atom(
                send_pair.at[k, lax.rem(me + q, n_atom)],
                recv_pair.at[k, q - 1],
                q,
                pair_send.at[k],
                pair_recv.at[k],
            ).start()
            return carry

        lax.fori_loop(1, n_atom, send, 0)

    build(0)
    for c in range(3):
        eig_t[HALF : HALF + MODE_DEV, c * ATOM_DEV : (c + 1) * ATOM_DEV] = eig[c].T

    @pl.when(block > 0)
    def _():
        up_cols.wait_recv()

    @pl.when(block == 0)
    def _():
        low_cols[...] = jnp.zeros_like(low_cols)

    @pl.when(block < n_mode - 1)
    def _():
        down_cols.wait_recv()

    @pl.when(block == n_mode - 1)
    def _():
        high_cols[...] = jnp.zeros_like(high_cols)

    for c in range(3):
        eig_t[:HALF, c * ATOM_DEV : (c + 1) * ATOM_DEV] = low_cols[c].T
        eig_t[HALF + MODE_DEV :, c * ATOM_DEV : (c + 1) * ATOM_DEV] = high_cols[c].T
    up_rows.wait_recv()
    down_rows.wait_recv()
    project(0)
    build(1)
    project(1)
    build(2)
    project(2)

    loads[4].wait()
    pltpu.make_async_copy(
        spectrum.at[pl.ds(1, n_mode - 1), :], spectrum.at[pl.ds(1, n_mode - 1), :], freq_recv
    ).wait()
    own_freq = spectrum[pl.ds(0, 1), :]
    columns = spectrum[...].T
    freq_col[:HALF] = jnp.broadcast_to(columns[HALF:, 1:2], (HALF, HALF))
    freq_col[HALF : HALF + MODE_DEV] = jnp.broadcast_to(columns[:, 0:1], (MODE_DEV, HALF))
    freq_col[HALF + MODE_DEV :] = jnp.broadcast_to(
        columns[:HALF, n_mode - 1 : n_mode], (HALF, HALF)
    )
    every = spectrum[...]
    highest = jnp.max(jnp.max(every, axis=1, keepdims=True), axis=0, keepdims=True)
    lowest = jnp.min(jnp.min(every, axis=1, keepdims=True), axis=0, keepdims=True)
    broaden = BROAD * (highest - lowest) / (n_mode * MODE_DEV - 1)

    start = block * MODE_DEV
    first = me * ROWS
    rows = first + iota((ROWS, HALF), 0)
    lanes = iota((ROWS, HALF), 1)
    weights = []
    for h in range(2):
        ours = slice(h * HALF, (h + 1) * HALF)
        mine = own_freq[:, ours]
        lower = band[0:1, ours]
        upper = band[1:2, ours]

        def freq_at(offset):
            return freq_col[pl.ds(pl.multiple_of(offset + first, ROWS), ROWS), :]

        before = freq_at(h * HALF)
        level = freq_at((h + 1) * HALF)
        after = freq_at((h + 2) * HALF)
        base = start + h * HALF + rows
        for partner, ids in (
            (
                jnp.where(rows > lanes, before, after),
                base + jnp.where(rows > lanes, -HALF, HALF),
            ),
            (
                jnp.where(rows == lanes, before, level),
                base + jnp.where(rows == lanes, -HALF, 0),
            ),
        ):
            own_ids = start + h * HALF + lanes
            inside = (ids >= lower) & (ids < upper) & (ids != own_ids)
            detune = mine - partner
            lorentz = broaden / math.pi / (detune * detune + broaden * broaden)
            factor = (mine + partner) ** 2 / (4.0 * mine * partner)
            weights.append((inside, lorentz * factor))

    strength = jnp.zeros((4, ROWS, HALF), F32)
    for k in range(3):
        pltpu.make_async_copy(recv_pair.at[k], recv_pair.at[k], pair_recv.at[k]).wait()
        total = send_pair[k, me]
        for q in range(n_atom - 1):
            total = total + recv_pair[k, q]
        strength = strength + total * total

    for h in range(2):
        term = 0.0
        for s in range(2):
            inside, weight = weights[2 * h + s]
            term = term + jnp.where(inside, weight * strength[2 * h + s], 0.0)
        send_sum[h : h + 1] = jnp.sum(term, axis=0, keepdims=True)

    def share(q, carry):
        to_atom(send_sum, recv_sum.at[q - 1], q, sum_send, sum_recv).start()
        return carry

    lax.fori_loop(1, n_atom, share, 0)
    freq_two = jnp.concatenate([own_freq[:, :HALF], own_freq[:, HALF:]], axis=0)
    grown = jnp.exp(freq_two)
    capacity = freq_two * freq_two * grown / ((grown - 1.0) * (grown - 1.0))
    prefactor = math.pi / (3.0 * freq_two * freq_two)
    pltpu.make_async_copy(recv_sum, recv_sum, sum_recv).wait()
    row_sums = send_sum[...]
    for q in range(n_atom - 1):
        row_sums = row_sums + recv_sum[q]
    diffusivity = prefactor * row_sums
    diff_ref[...] = diffusivity
    running = capacity * diffusivity
    send_total[...] = jnp.broadcast_to(
        jnp.sum(jnp.sum(running, axis=1, keepdims=True), axis=0, keepdims=True), (1, HALF)
    )

    def share_total(q, carry):
        to_mode(send_total, recv_total.at[q - 1], q, total_send, total_recv).start()
        return carry

    lax.fori_loop(1, n_mode, share_total, 0)
    lane_two = iota((2, HALF), 1)
    for step in (1, 2, 4, 8, 16, 32, 64):
        running = running + jnp.where(lane_two >= step, pltpu.roll(running, step, 1), 0.0)
    low_total = running[0:1, HALF - 1 : HALF]
    running = running + jnp.where(iota((2, HALF), 0) == 1, low_total, 0.0)
    pltpu.make_async_copy(recv_total, recv_total, total_recv).wait()
    earlier = jnp.zeros((1, HALF), F32)
    for q in range(1, n_mode):
        earlier = earlier + jnp.where(block >= q, recv_total[q - 1], 0.0)
    cond_ref[...] = (earlier + running) / MODE_DEV

    up_rows.wait_send()
    down_rows.wait_send()

    @pl.when(block < n_mode - 1)
    def _():
        up_cols.wait_send()

    @pl.when(block > 0)
    def _():
        down_cols.wait_send()

    pltpu.make_async_copy(
        spectrum.at[pl.ds(1, n_mode - 1), :], spectrum.at[pl.ds(1, n_mode - 1), :], freq_send
    ).wait()
    for k in range(3):
        pltpu.make_async_copy(recv_pair.at[k], recv_pair.at[k], pair_send.at[k]).wait()
    pltpu.make_async_copy(recv_sum, recv_sum, sum_send).wait()
    pltpu.make_async_copy(recv_total, recv_total, total_send).wait()


def body(eigvec, force, bond, nbr, band, freq):
    n_atom, n_mode = lax.axis_size("atom"), lax.axis_size("mode")
    any_spec = pl.BlockSpec(memory_space=pl.ANY)
    vmem_spec = pl.BlockSpec(memory_space=pltpu.VMEM)
    dma = pltpu.SemaphoreType.DMA
    diffusivity, conductivity = pl.pallas_call(
        functools.partial(kernel, n_atom, n_mode),
        out_shape=(
            jax.ShapeDtypeStruct((2, HALF), F32),
            jax.ShapeDtypeStruct((2, HALF), F32),
        ),
        in_specs=[any_spec] * 6,
        out_specs=(vmem_spec, vmem_spec),
        scratch_shapes=[
            pltpu.VMEM((3, ATOM_DEV, MODE_DEV), BF16),
            pltpu.VMEM((3, 3, NBR, ATOM_DEV), F32),
            pltpu.VMEM((3, NBR, ATOM_DEV), F32),
            pltpu.VMEM((NBR, ATOM_DEV), jnp.int32),
            pltpu.VMEM((2, MODE_DEV), jnp.int32),
            pltpu.VMEM((n_mode, MODE_DEV), F32),
            pltpu.VMEM((3, RIM, MODE_DEV), BF16),
            pltpu.VMEM((3, RIM, MODE_DEV), BF16),
            pltpu.VMEM((3, ATOM_DEV, HALF), BF16),
            pltpu.VMEM((3, ATOM_DEV, HALF), BF16),
            pltpu.VMEM((GROUPS, 256), F32),
            pltpu.VMEM((GROUPS, REACH, 256), BF16),
            pltpu.VMEM((GROUPS, 9 * GROUP, 256), BF16),
            pltpu.VMEM((3, ATOM_DEV, 3 * ATOM_DEV), BF16),
            pltpu.VMEM((3, ATOM_DEV, 3 * RIM), BF16),
            pltpu.VMEM((3, ATOM_DEV, MODE_DEV), BF16),
            pltpu.VMEM((MODE_DEV + 2 * HALF, 3 * ATOM_DEV), BF16),
            pltpu.VMEM((3, n_atom, 4, ROWS, HALF), F32),
            pltpu.VMEM((3, n_atom - 1, 4, ROWS, HALF), F32),
            pltpu.VMEM((MODE_DEV + 2 * HALF, HALF), F32),
            pltpu.VMEM((2, HALF), F32),
            pltpu.VMEM((n_atom - 1, 2, HALF), F32),
            pltpu.VMEM((1, HALF), F32),
            pltpu.VMEM((n_mode - 1, 1, HALF), F32),
            dma((6,)),
            dma((2,)),
            dma((2,)),
            dma((2,)),
            dma((2,)),
            dma(()),
            dma(()),
            dma((3,)),
            dma((3,)),
            dma(()),
            dma(()),
            dma(()),
            dma(()),
        ],
        compiler_params=pltpu.CompilerParams(
            collective_id=0, has_side_effects=True, vmem_limit_bytes=63 * 1024 * 1024
        ),
    )(eigvec, force, bond, nbr, band, freq.reshape(1, MODE_DEV))
    return diffusivity.reshape(MODE_DEV), conductivity.reshape(MODE_DEV)


def solution(mesh):
    in_specs = (
        P(None, "atom", "mode"),
        P(None, None, None, "atom"),
        P(None, None, "atom"),
        P(None, "atom"),
        P(None, "mode"),
        P("mode"),
    )
    out_specs = (P("mode"), P("mode"))
    return jax.shard_map(body, mesh=mesh, in_specs=in_specs, out_specs=out_specs, check_vma=False)
```

time: 191 us -> 46.1 us (0.24)
  the two profiles are of different devices: /device:TPU:97 before, /device:TPU:1 now
where the time goes in v1:
time: 46.1 us; the launch traced here: 45.9 us
  Pallas kernels  43.4 us (94%)
  local copies, waits for them, and re-layouts  1.86 us (4%)
  between operations  0.65 us (1%)
    pallas_call x1, Pallas kernels, body(): pl.pallas_call(functools.partial(kernel, n_atom, n_mode), out_shape=(jax....  43.4 us
    unnamed x6, local copies, waits for them, and re-layouts  1.86 us

profile of v1, /device:TPU:1, one launch (start us, length us, event | category | flops | bytes accessed | tf_op | source)
XLA Modules:
  0.0 45.9 jit_solution(5798677842686872939)
XLA Ops:
  0.6 43.4 %shard_map.77 = (f32[2,128]{1,0:T(2,128)}, f32[2,128]{1,0:T(2,128)}) custom-call(bf16[3,256,256]{2,1,0:T(8,128)(2,1)} %eig_hbm.1, f32[3,3,16,256]{3,2,1,0:T(8,128)} %force_hbm.1, f32[3,16,256]{2,1,0:T(8,128)} %bond_hbm.1, s32[16,256]{1,0:T(8,128)} %nbr_hbm.1, s32[2,256]{1,0:T(2,128)} %band_hbm.1, f32[1,256]{1,0:T(1,128)} %bitcast.3), custom_call_target="tpu_custom_call" | custom-call | tf_op jit(solution)/shard_map/pallas_call | solution.py:423
  44.0 0.0 copy-start.1
  44.0 0.7 %copy-done.1 = f32[2,128]{1,0:T(2,128)S(1)} copy-done((f32[2,128]{1,0:T(2,128)S(1)}, f32[2,128]{1,0:T(2,128)}, u32[]{:S(2)}) %copy-start.1) | copy-done | bytes 1048
  44.7 0.0 copy-start
  44.7 0.6 %copy.10 = f32[256]{0:T(256)} copy(f32[256]{0:T(256)S(1)} %bitcast.5) | data formatting | bytes 2048
  45.3 0.1 copy-done
  45.3 0.6 %copy.11 = f32[256]{0:T(256)} copy(f32[256]{0:T(256)S(1)} %bitcast.4) | data formatting | bytes 2048
Async XLA Ops:
  44.0 0.7 %copy-start.1 = (f32[2,128]{1,0:T(2,128)S(1)}, f32[2,128]{1,0:T(2,128)}, u32[]{:S(2)}) copy-start(f32[2,128]{1,0:T(2,128)} %get-tuple-element.4) | copy-start | bytes 3076
  44.7 0.6 %copy-start = (f32[2,128]{1,0:T(2,128)S(1)}, f32[2,128]{1,0:T(2,128)}, u32[]{:S(2)}) copy-start(f32[2,128]{1,0:T(2,128)} %get-tuple-element.5) | copy-start | bytes 3076

commit v2 on v1

--- a/solution.py
+++ b/solution.py
@@ -16,7 +16,6 @@
 BROAD = 128
 GROUP = 16
 GROUPS = ATOM_DEV // GROUP
-REACH = ATOM_DEV + RIM
 ROWS = 8
 BF16 = jnp.bfloat16
 F32 = jnp.float32
@@ -31,6 +30,10 @@
     return lax.dot_general(
         lhs, rhs, (((lhs_dim,), (rhs_dim,)), ((), ())), preferred_element_type=F32
     )
+
+
+def drain(ref, sem):
+    pltpu.make_async_copy(ref, ref, sem).wait()
 
 
 def kernel(
@@ -54,7 +57,7 @@
     high_rows,
     low_cols,
     high_cols,
-    nbr_rows,
+    nbr_cols,
     hot,
     spread,
     own_m,
@@ -121,12 +124,10 @@
     ).astype(BF16)
 
     loads[0].wait()
-    place = ((nbr[...] - me * ATOM_DEV + RIM + atoms) & (atoms - 1)) - RIM
-    column = jnp.where(place < 0, place + REACH, place)
-    coarse = contract((column >> 4).astype(F32).astype(BF16), slot_rows, 0, 0)
-    fine = contract((column & 15).astype(F32).astype(BF16), slot_rows, 0, 0)
-    column_of = jnp.where(diagonal, coarse * 16.0 + fine, 0.0)
-    nbr_rows[...] = jnp.sum(column_of.reshape(GROUPS, GROUP, 256), axis=1)
+    atom_ids = iota((NBR, ATOM_DEV), 1)
+    offset = ((nbr[...] - me * ATOM_DEV - atom_ids + RIM + atoms) & (atoms - 1)) - RIM
+    column = jnp.where(offset == RIM, atom_ids, (atom_ids + offset) & (ATOM_DEV - 1))
+    nbr_cols[...] = column.astype(F32).T
 
     loads[5].wait()
     loads[3].wait()
@@ -187,10 +188,14 @@
 
     lax.fori_loop(1, n_mode, send_freq, 0)
 
-    reach_rows = iota((REACH, 256), 0).astype(F32)
+    col_ids = iota((GROUP, ATOM_DEV), 1).astype(F32)
 
     def one_hot(g, carry):
-        hot[g] = jnp.where(reach_rows == nbr_rows[pl.ds(g, 1), :], 1.0, 0.0).astype(BF16)
+        own_cols = nbr_cols[pl.ds(pl.multiple_of(g * GROUP, GROUP), GROUP), :]
+        for n in range(NBR):
+            hot[g, n * GROUP : (n + 1) * GROUP, :] = jnp.where(
+                own_cols[:, n : n + 1] == col_ids, 1.0, 0.0
+            ).astype(BF16)
         return carry
 
     lax.fori_loop(0, GROUPS, one_hot, 0)
@@ -198,40 +203,63 @@
     loads[1].wait()
     loads[2].wait()
 
-    def build(k):
-        for c in range(3):
-            for d in range(3):
-                coupling = (bond[k] * force[c, d]).astype(BF16)
-                wide = jnp.where(diagonal, contract(coupling, slot_rows, 0, 0), 0.0).astype(BF16)
-                first = (3 * c + d) * GROUP
-                spread[:, first : first + GROUP, :] = wide.reshape(GROUPS, GROUP, 256)
-
-        def group(g, carry):
-            dense = contract(spread[g], hot[g], 1, 1).astype(BF16)
+    def spread_out():
+        for k in range(3):
             for c in range(3):
                 for d in range(3):
-                    first = (3 * c + d) * GROUP
-                    part = dense[first : first + GROUP]
-                    rows = pl.ds(pl.multiple_of(g * GROUP, GROUP), GROUP)
-                    own_m[c, rows, d * ATOM_DEV : (d + 1) * ATOM_DEV] = part[:, :ATOM_DEV]
-                    rim_m[c, rows, d * RIM : (d + 1) * RIM] = part[:, ATOM_DEV:]
-            return carry
-
-        lax.fori_loop(0, GROUPS, group, 0)
+                    coupling = (bond[k] * force[c, d]).astype(BF16)
+                    wide = jnp.where(diagonal, contract(coupling, slot_rows, 0, 0), 0.0)
+                    first = (9 * k + 3 * c + d) * GROUP
+                    spread[:, first : first + GROUP, :] = wide.astype(BF16).reshape(
+                        GROUPS, GROUP, 256
+                    )
+
+    near = iota((GROUP, RIM), 1) - iota((GROUP, RIM), 0)
+
+    def unfold(h, g):
+        dense = contract(spread[g], hot[g], 1, 0)
+        gap = near - (g - h * (GROUPS // 2)) * GROUP
+        below, same = gap < 0, gap == 0
+        rows = pl.ds(pl.multiple_of(g * GROUP, GROUP), GROUP)
+        for q in range(9):
+            for d in range(3):
+                first = (3 * q + d) * GROUP
+                left = dense[first : first + GROUP, :RIM]
+                right = dense[first : first + GROUP, RIM:]
+                if h == 0:
+                    own_left = jnp.where(same, 0.0, left)
+                    own_right = jnp.where(below, right, jnp.where(same, left, 0.0))
+                    rim = jnp.where(below, 0.0, right)
+                else:
+                    own_left = jnp.where(below, 0.0, left)
+                    own_right = jnp.where(same, 0.0, right)
+                    rim = jnp.where(below, left, jnp.where(same, right, 0.0))
+                own_m[q, rows, d * ATOM_DEV : d * ATOM_DEV + RIM] = own_left.astype(BF16)
+                own_m[q, rows, d * ATOM_DEV + RIM : (d + 1) * ATOM_DEV] = own_right.astype(BF16)
+                rim_m[q, rows, d * RIM : (d + 1) * RIM] = rim.astype(BF16)
+
+    def build():
+        for h in range(2):
+
+            def group(g, carry, h=h):
+                unfold(h, g)
+                return carry
+
+            lax.fori_loop(h * (GROUPS // 2), (h + 1) * (GROUPS // 2), group, 0)
 
     row = iota((HALF, HALF), 0)
     col = iota((HALF, HALF), 1)
 
     def project(k):
         inner = contract(
-            own_m[...].reshape(3 * ATOM_DEV, 3 * ATOM_DEV),
+            own_m[3 * k : 3 * k + 3].reshape(3 * ATOM_DEV, 3 * ATOM_DEV),
             eig[...].reshape(3 * ATOM_DEV, MODE_DEV),
             1,
             0,
         ).reshape(3, ATOM_DEV, MODE_DEV)
         for h, halo in enumerate((low_rows, high_rows)):
             outer = contract(
-                rim_m[:, h * RIM : (h + 1) * RIM, :].reshape(3 * RIM, 3 * RIM),
+                rim_m[3 * k : 3 * k + 3, h * RIM : (h + 1) * RIM, :].reshape(3 * RIM, 3 * RIM),
                 halo[...].reshape(3 * RIM, MODE_DEV),
                 1,
                 0,
@@ -262,7 +290,8 @@
 
         lax.fori_loop(1, n_atom, send, 0)
 
-    build(0)
+    spread_out()
+    build()
     for c in range(3):
         eig_t[HALF : HALF + MODE_DEV, c * ATOM_DEV : (c + 1) * ATOM_DEV] = eig[c].T
 
@@ -288,15 +317,11 @@
     up_rows.wait_recv()
     down_rows.wait_recv()
     project(0)
-    build(1)
     project(1)
-    build(2)
     project(2)
 
     loads[4].wait()
-    pltpu.make_async_copy(
-        spectrum.at[pl.ds(1, n_mode - 1), :], spectrum.at[pl.ds(1, n_mode - 1), :], freq_recv
-    ).wait()
+    drain(spectrum.at[pl.ds(1, n_mode - 1), :], freq_recv)
     own_freq = spectrum[pl.ds(0, 1), :]
     columns = spectrum[...].T
     freq_col[:HALF] = jnp.broadcast_to(columns[HALF:, 1:2], (HALF, HALF))
@@ -346,7 +371,7 @@
 
     strength = jnp.zeros((4, ROWS, HALF), F32)
     for k in range(3):
-        pltpu.make_async_copy(recv_pair.at[k], recv_pair.at[k], pair_recv.at[k]).wait()
+        drain(recv_pair.at[k], pair_recv.at[k])
         total = send_pair[k, me]
         for q in range(n_atom - 1):
             total = total + recv_pair[k, q]
@@ -368,7 +393,7 @@
     grown = jnp.exp(freq_two)
     capacity = freq_two * freq_two * grown / ((grown - 1.0) * (grown - 1.0))
     prefactor = math.pi / (3.0 * freq_two * freq_two)
-    pltpu.make_async_copy(recv_sum, recv_sum, sum_recv).wait()
+    drain(recv_sum, sum_recv)
     row_sums = send_sum[...]
     for q in range(n_atom - 1):
         row_sums = row_sums + recv_sum[q]
@@ -389,7 +414,7 @@
         running = running + jnp.where(lane_two >= step, pltpu.roll(running, step, 1), 0.0)
     low_total = running[0:1, HALF - 1 : HALF]
     running = running + jnp.where(iota((2, HALF), 0) == 1, low_total, 0.0)
-    pltpu.make_async_copy(recv_total, recv_total, total_recv).wait()
+    drain(recv_total, total_recv)
     earlier = jnp.zeros((1, HALF), F32)
     for q in range(1, n_mode):
         earlier = earlier + jnp.where(block >= q, recv_total[q - 1], 0.0)
@@ -406,13 +431,11 @@
     def _():
         down_cols.wait_send()
 
-    pltpu.make_async_copy(
-        spectrum.at[pl.ds(1, n_mode - 1), :], spectrum.at[pl.ds(1, n_mode - 1), :], freq_send
-    ).wait()
+    drain(spectrum.at[pl.ds(1, n_mode - 1), :], freq_send)
     for k in range(3):
-        pltpu.make_async_copy(recv_pair.at[k], recv_pair.at[k], pair_send.at[k]).wait()
-    pltpu.make_async_copy(recv_sum, recv_sum, sum_send).wait()
-    pltpu.make_async_copy(recv_total, recv_total, total_send).wait()
+        drain(recv_pair.at[k], pair_send.at[k])
+    drain(recv_sum, sum_send)
+    drain(recv_total, total_send)
 
 
 def body(eigvec, force, bond, nbr, band, freq):
@@ -439,11 +462,11 @@
             pltpu.VMEM((3, RIM, MODE_DEV), BF16),
             pltpu.VMEM((3, ATOM_DEV, HALF), BF16),
             pltpu.VMEM((3, ATOM_DEV, HALF), BF16),
-            pltpu.VMEM((GROUPS, 256), F32),
-            pltpu.VMEM((GROUPS, REACH, 256), BF16),
-            pltpu.VMEM((GROUPS, 9 * GROUP, 256), BF16),
-            pltpu.VMEM((3, ATOM_DEV, 3 * ATOM_DEV), BF16),
-            pltpu.VMEM((3, ATOM_DEV, 3 * RIM), BF16),
+            pltpu.VMEM((ATOM_DEV, NBR), F32),
+            pltpu.VMEM((GROUPS, 256, ATOM_DEV), BF16),
+            pltpu.VMEM((GROUPS, 27 * GROUP, 256), BF16),
+            pltpu.VMEM((9, ATOM_DEV, 3 * ATOM_DEV), BF16),
+            pltpu.VMEM((9, ATOM_DEV, 3 * RIM), BF16),
             pltpu.VMEM((3, ATOM_DEV, MODE_DEV), BF16),
             pltpu.VMEM((MODE_DEV + 2 * HALF, 3 * ATOM_DEV), BF16),
             pltpu.VMEM((3, n_atom, 4, ROWS, HALF), F32),

time: 46.1 us -> 40.2 us (0.87)
  Pallas kernels: 43.4 us -> 37.5 us
    pallas_call x1, Pallas kernels: 43.4 us -> 37.5 us  [body(): pl.pallas_call(functools.partial(kernel, n_atom, n_mode), out_shape=(jax....]
where the time goes in v2:
time: 40.2 us; the launch traced here: 40 us
  Pallas kernels  37.5 us (93%)
  local copies, waits for them, and re-layouts  1.86 us (5%)
  between operations  0.65 us (2%)
    pallas_call x1, Pallas kernels, body(): pl.pallas_call(functools.partial(kernel, n_atom, n_mode), out_shape=(jax....  37.5 us
    unnamed x6, local copies, waits for them, and re-layouts  1.86 us

profile of v2, /device:TPU:1, one launch (start us, length us, event | category | flops | bytes accessed | tf_op | source)
XLA Modules:
  0.0 40.0 jit_solution(14783961238942559166)
XLA Ops:
  0.6 37.5 %shard_map.77 = (f32[2,128]{1,0:T(2,128)}, f32[2,128]{1,0:T(2,128)}) custom-call(bf16[3,256,256]{2,1,0:T(8,128)(2,1)} %eig_hbm.1, f32[3,3,16,256]{3,2,1,0:T(8,128)} %force_hbm.1, f32[3,16,256]{2,1,0:T(8,128)} %bond_hbm.1, s32[16,256]{1,0:T(8,128)} %nbr_hbm.1, s32[2,256]{1,0:T(2,128)} %band_hbm.1, f32[1,256]{1,0:T(1,128)} %bitcast.3), custom_call_target="tpu_custom_call" | custom-call | tf_op jit(solution)/shard_map/pallas_call | solution.py:446
  38.1 0.0 copy-start.1
  38.1 0.7 %copy-done.1 = f32[2,128]{1,0:T(2,128)S(1)} copy-done((f32[2,128]{1,0:T(2,128)S(1)}, f32[2,128]{1,0:T(2,128)}, u32[]{:S(2)}) %copy-start.1) | copy-done | bytes 1048
  38.8 0.0 copy-start
  38.8 0.6 %copy.10 = f32[256]{0:T(256)} copy(f32[256]{0:T(256)S(1)} %bitcast.5) | data formatting | bytes 2048
  39.3 0.1 copy-done
  39.4 0.6 %copy.11 = f32[256]{0:T(256)} copy(f32[256]{0:T(256)S(1)} %bitcast.4) | data formatting | bytes 2048
Async XLA Ops:
  38.1 0.7 %copy-start.1 = (f32[2,128]{1,0:T(2,128)S(1)}, f32[2,128]{1,0:T(2,128)}, u32[]{:S(2)}) copy-start(f32[2,128]{1,0:T(2,128)} %get-tuple-element.4) | copy-start | bytes 3076
  38.8 0.6 %copy-start = (f32[2,128]{1,0:T(2,128)S(1)}, f32[2,128]{1,0:T(2,128)}, u32[]{:S(2)}) copy-start(f32[2,128]{1,0:T(2,128)} %get-tuple-element.5) | copy-start | bytes 3076

commit v3 on v2

--- a/solution.py
+++ b/solution.py
@@ -71,6 +71,7 @@
     recv_sum,
     send_total,
     recv_total,
+    inner_flux,
     local_sem,
     row_send,
     row_recv,
@@ -84,6 +85,7 @@
     sum_recv,
     total_send,
     total_recv,
+    ready,
 ):
     me = lax.axis_index("atom")
     block = lax.axis_index("mode")
@@ -97,14 +99,22 @@
         )
         return carry
 
-    def greet_mode(q, carry):
-        pl.semaphore_signal(
-            barrier, inc=1, device_id=(me, lax.rem(block + q, n_mode)), device_id_type=MESH
-        )
-        return carry
-
+    recv_total[...] = jnp.zeros_like(recv_total)
     lax.fori_loop(1, n_atom, greet_atom, 0)
-    lax.fori_loop(1, n_mode, greet_mode, 0)
+
+    def beside(shift, action):
+        @pl.when(block + shift < n_mode)
+        def _():
+            action(block + shift)
+
+        @pl.when(block - shift >= 0)
+        def _():
+            action(block - shift)
+
+    def greet_mode(other):
+        pl.semaphore_signal(barrier, inc=1, device_id=(me, other), device_id_type=MESH)
+
+    beside(1, greet_mode)
 
     loads = [
         pltpu.make_async_copy(nbr_hbm, nbr, local_sem.at[0]),
@@ -129,9 +139,24 @@
     column = jnp.where(offset == RIM, atom_ids, (atom_ids + offset) & (ATOM_DEV - 1))
     nbr_cols[...] = column.astype(F32).T
 
+    col_ids = iota((GROUP, ATOM_DEV), 1).astype(F32)
+
+    def one_hot(g, carry):
+        own_cols = nbr_cols[pl.ds(pl.multiple_of(g * GROUP, GROUP), GROUP), :]
+        for n in range(NBR):
+            hot[g, n * GROUP : (n + 1) * GROUP, :] = jnp.where(
+                own_cols[:, n : n + 1] == col_ids, 1.0, 0.0
+            ).astype(BF16)
+        return carry
+
+    lax.fori_loop(0, GROUPS, one_hot, 0)
+
     loads[5].wait()
     loads[3].wait()
-    pl.semaphore_wait(barrier, n_atom + n_mode - 2)
+    pl.semaphore_wait(
+        barrier,
+        n_atom - 1 + (block > 0).astype(jnp.int32) + (block < n_mode - 1).astype(jnp.int32),
+    )
 
     def to_atom(src, dst, q, send, recv):
         return pltpu.make_async_remote_copy(
@@ -176,6 +201,22 @@
     def _():
         down_cols.start()
 
+    @pl.when(block > 0)
+    def _():
+        pl.semaphore_wait(ready.at[0], 1)
+
+    @pl.when(block < n_mode - 1)
+    def _():
+        pl.semaphore_signal(
+            ready.at[0], inc=1, device_id=(me, block + 1), device_id_type=MESH
+        )
+
+    def tell(other, carry):
+        pl.semaphore_signal(ready.at[1], inc=1, device_id=(me, other), device_id_type=MESH)
+        return carry
+
+    lax.fori_loop(0, block, tell, 0)
+
     def send_freq(q, carry):
         to_mode(
             spectrum.at[pl.ds(0, 1), :],
@@ -186,19 +227,7 @@
         ).start()
         return carry
 
-    lax.fori_loop(1, n_mode, send_freq, 0)
-
-    col_ids = iota((GROUP, ATOM_DEV), 1).astype(F32)
-
-    def one_hot(g, carry):
-        own_cols = nbr_cols[pl.ds(pl.multiple_of(g * GROUP, GROUP), GROUP), :]
-        for n in range(NBR):
-            hot[g, n * GROUP : (n + 1) * GROUP, :] = jnp.where(
-                own_cols[:, n : n + 1] == col_ids, 1.0, 0.0
-            ).astype(BF16)
-        return carry
-
-    lax.fori_loop(0, GROUPS, one_hot, 0)
+    lax.fori_loop(n_mode - block, n_mode, send_freq, 0)
 
     loads[1].wait()
     loads[2].wait()
@@ -250,13 +279,15 @@
     row = iota((HALF, HALF), 0)
     col = iota((HALF, HALF), 1)
 
-    def project(k):
-        inner = contract(
+    def inner_part_of(k):
+        inner_flux[3 * k : 3 * k + 3] = contract(
             own_m[3 * k : 3 * k + 3].reshape(3 * ATOM_DEV, 3 * ATOM_DEV),
             eig[...].reshape(3 * ATOM_DEV, MODE_DEV),
             1,
             0,
         ).reshape(3, ATOM_DEV, MODE_DEV)
+
+    def project(k):
         for h, halo in enumerate((low_rows, high_rows)):
             outer = contract(
                 rim_m[3 * k : 3 * k + 3, h * RIM : (h + 1) * RIM, :].reshape(3 * RIM, 3 * RIM),
@@ -265,7 +296,7 @@
                 0,
             ).reshape(3, RIM, MODE_DEV)
             flux[:, h * RIM : (h + 1) * RIM, :] = (
-                inner[:, h * RIM : (h + 1) * RIM, :] + outer
+                inner_flux[3 * k : 3 * k + 3, h * RIM : (h + 1) * RIM, :] + outer
             ).astype(BF16)
         pair = contract(eig_t[...], flux[...].reshape(3 * ATOM_DEV, MODE_DEV), 1, 0)
         for h in range(2):
@@ -292,6 +323,8 @@
 
     spread_out()
     build()
+    for k in range(3):
+        inner_part_of(k)
     for c in range(3):
         eig_t[HALF : HALF + MODE_DEV, c * ATOM_DEV : (c + 1) * ATOM_DEV] = eig[c].T
 
@@ -318,6 +351,12 @@
     down_rows.wait_recv()
     project(0)
     project(1)
+
+    @pl.when(block < n_mode - 1)
+    def _():
+        pl.semaphore_wait(ready.at[1], n_mode - 1 - block)
+
+    lax.fori_loop(1, n_mode - block, send_freq, 0)
     project(2)
 
     loads[4].wait()
@@ -393,32 +432,51 @@
     grown = jnp.exp(freq_two)
     capacity = freq_two * freq_two * grown / ((grown - 1.0) * (grown - 1.0))
     prefactor = math.pi / (3.0 * freq_two * freq_two)
+    part_total = capacity * prefactor * send_sum[...]
+    send_total[...] = part_total[0:1] + part_total[1:2]
+
+    def share_total(t, carry):
+        shift = n_mode - 1 - block - t
+
+        def share_to(q, carry):
+            pltpu.make_async_remote_copy(
+                src_ref=send_total,
+                dst_ref=recv_total.at[shift - 1, q],
+                send_sem=total_send.at[shift - 1],
+                recv_sem=total_recv.at[shift - 1],
+                device_id=(lax.rem(me + q, n_atom), block + shift),
+                device_id_type=MESH,
+            ).start()
+            return carry
+
+        return lax.fori_loop(0, n_atom, share_to, carry, unroll=True)
+
+    lax.fori_loop(0, n_mode - 1 - block, share_total, 0)
     drain(recv_sum, sum_recv)
     row_sums = send_sum[...]
     for q in range(n_atom - 1):
         row_sums = row_sums + recv_sum[q]
     diffusivity = prefactor * row_sums
-    diff_ref[...] = diffusivity
+    diff_ref[:, :HALF] = diffusivity[0:1]
+    diff_ref[:, HALF:] = diffusivity[1:2]
     running = capacity * diffusivity
-    send_total[...] = jnp.broadcast_to(
-        jnp.sum(jnp.sum(running, axis=1, keepdims=True), axis=0, keepdims=True), (1, HALF)
-    )
-
-    def share_total(q, carry):
-        to_mode(send_total, recv_total.at[q - 1], q, total_send, total_recv).start()
-        return carry
-
-    lax.fori_loop(1, n_mode, share_total, 0)
     lane_two = iota((2, HALF), 1)
     for step in (1, 2, 4, 8, 16, 32, 64):
         running = running + jnp.where(lane_two >= step, pltpu.roll(running, step, 1), 0.0)
     low_total = running[0:1, HALF - 1 : HALF]
     running = running + jnp.where(iota((2, HALF), 0) == 1, low_total, 0.0)
-    drain(recv_total, total_recv)
-    earlier = jnp.zeros((1, HALF), F32)
-    for q in range(1, n_mode):
-        earlier = earlier + jnp.where(block >= q, recv_total[q - 1], 0.0)
-    cond_ref[...] = (earlier + running) / MODE_DEV
+
+    def hear_total(t, carry):
+        drain(recv_total.at[t], total_recv.at[t])
+        return carry
+
+    lax.fori_loop(0, block, hear_total, 0)
+    earlier = jnp.sum(
+        jnp.sum(jnp.sum(recv_total[...], axis=(0, 1)), axis=0, keepdims=True), axis=1, keepdims=True
+    )
+    conductivity = (earlier + running) / MODE_DEV
+    cond_ref[:, :HALF] = conductivity[0:1]
+    cond_ref[:, HALF:] = conductivity[1:2]
 
     up_rows.wait_send()
     down_rows.wait_send()
@@ -435,7 +493,12 @@
     for k in range(3):
         drain(recv_pair.at[k], pair_send.at[k])
     drain(recv_sum, sum_send)
-    drain(recv_total, total_send)
+
+    def sent_total(t, carry):
+        drain(recv_total.at[t], total_send.at[t])
+        return carry
+
+    lax.fori_loop(0, n_mode - 1 - block, sent_total, 0)
 
 
 def body(eigvec, force, bond, nbr, band, freq):
@@ -446,8 +509,8 @@
     diffusivity, conductivity = pl.pallas_call(
         functools.partial(kernel, n_atom, n_mode),
         out_shape=(
-            jax.ShapeDtypeStruct((2, HALF), F32),
-            jax.ShapeDtypeStruct((2, HALF), F32),
+            jax.ShapeDtypeStruct((1, MODE_DEV), F32),
+            jax.ShapeDtypeStruct((1, MODE_DEV), F32),
         ),
         in_specs=[any_spec] * 6,
         out_specs=(vmem_spec, vmem_spec),
@@ -475,7 +538,8 @@
             pltpu.VMEM((2, HALF), F32),
             pltpu.VMEM((n_atom - 1, 2, HALF), F32),
             pltpu.VMEM((1, HALF), F32),
-            pltpu.VMEM((n_mode - 1, 1, HALF), F32),
+            pltpu.VMEM((n_mode - 1, n_atom, 1, HALF), F32),
+            pltpu.VMEM((9, ATOM_DEV, MODE_DEV), F32),
             dma((6,)),
             dma((2,)),
             dma((2,)),
@@ -487,8 +551,9 @@
             dma((3,)),
             dma(()),
             dma(()),
-            dma(()),
-            dma(()),
+            dma((n_mode - 1,)),
+            dma((n_mode - 1,)),
+            pltpu.SemaphoreType.REGULAR((2,)),
         ],
         compiler_params=pltpu.CompilerParams(
             collective_id=0, has_side_effects=True, vmem_limit_bytes=63 * 1024 * 1024

time: 40.2 us -> 35.8 us (0.89)
  Pallas kernels: 37.5 us -> 33.1 us
    pallas_call x1, Pallas kernels: 37.5 us -> 33.1 us  [body(): pl.pallas_call(functools.partial(kernel, n_atom, n_mode), out_shape=(jax....]
where the time goes in v3:
time: 35.8 us; the launch traced here: 35.6 us
  Pallas kernels  33.1 us (92%)
  local copies, waits for them, and re-layouts  1.86 us (5%)
  between operations  0.65 us (2%)
    pallas_call x1, Pallas kernels, body(): pl.pallas_call(functools.partial(kernel, n_atom, n_mode), out_shape=(jax....  33.1 us
    unnamed x6, local copies, waits for them, and re-layouts  1.86 us

profile of v3, /device:TPU:1, one launch (start us, length us, event | category | flops | bytes accessed | tf_op | source)
XLA Modules:
  0.0 35.6 jit_solution(698196595200655511)
XLA Ops:
  0.6 33.1 %shard_map.77 = (f32[1,256]{1,0:T(1,128)}, f32[1,256]{1,0:T(1,128)}) custom-call(bf16[3,256,256]{2,1,0:T(8,128)(2,1)} %eig_hbm.1, f32[3,3,16,256]{3,2,1,0:T(8,128)} %force_hbm.1, f32[3,16,256]{2,1,0:T(8,128)} %bond_hbm.1, s32[16,256]{1,0:T(8,128)} %nbr_hbm.1, s32[2,256]{1,0:T(2,128)} %band_hbm.1, f32[1,256]{1,0:T(1,128)} %bitcast.3), custom_call_target="tpu_custom_call" | custom-call | tf_op jit(solution)/shard_map/pallas_call | solution.py:509
  33.7 0.0 copy-start.1
  33.7 0.7 %copy-done.1 = f32[1,256]{1,0:T(1,128)S(1)} copy-done((f32[1,256]{1,0:T(1,128)S(1)}, f32[1,256]{1,0:T(1,128)}, u32[]{:S(2)}) %copy-start.1) | copy-done | bytes 1048
  34.4 0.0 copy-start
  34.4 0.6 %copy.10 = f32[256]{0:T(256)} copy(f32[256]{0:T(256)S(1)} %bitcast.5) | data formatting | bytes 2048
  34.9 0.1 copy-done
  35.0 0.6 %copy.11 = f32[256]{0:T(256)} copy(f32[256]{0:T(256)S(1)} %bitcast.4) | data formatting | bytes 2048
Async XLA Ops:
  33.7 0.7 %copy-start.1 = (f32[1,256]{1,0:T(1,128)S(1)}, f32[1,256]{1,0:T(1,128)}, u32[]{:S(2)}) copy-start(f32[1,256]{1,0:T(1,128)} %get-tuple-element.4) | copy-start | bytes 3076
  34.4 0.6 %copy-start = (f32[1,256]{1,0:T(1,128)S(1)}, f32[1,256]{1,0:T(1,128)}, u32[]{:S(2)}) copy-start(f32[1,256]{1,0:T(1,128)} %get-tuple-element.5) | copy-start | bytes 3076

commit v4 on v3

--- a/solution.py
+++ b/solution.py
@@ -45,8 +45,7 @@
     nbr_hbm,
     band_hbm,
     freq_hbm,
-    diff_ref,
-    cond_ref,
+    out_ref,
     eig,
     force,
     bond,
@@ -149,7 +148,7 @@
             ).astype(BF16)
         return carry
 
-    lax.fori_loop(0, GROUPS, one_hot, 0)
+    lax.fori_loop(0, GROUPS, one_hot, 0, unroll=4)
 
     loads[5].wait()
     loads[3].wait()
@@ -274,7 +273,9 @@
                 unfold(h, g)
                 return carry
 
-            lax.fori_loop(h * (GROUPS // 2), (h + 1) * (GROUPS // 2), group, 0)
+            lax.fori_loop(
+                h * (GROUPS // 2), (h + 1) * (GROUPS // 2), group, 0, unroll=True
+            )
 
     row = iota((HALF, HALF), 0)
     col = iota((HALF, HALF), 1)
@@ -306,8 +307,8 @@
             after = pair[(h + 2) * HALF : (h + 3) * HALF, ours]
             outer = jnp.where(row > col, before, after)
             inner_part = jnp.where(row == col, before, level)
-            send_pair[k, :, 2 * h] = outer.reshape(n_atom, ROWS, HALF)
-            send_pair[k, :, 2 * h + 1] = inner_part.reshape(n_atom, ROWS, HALF)
+            send_pair[k, :, 2 * h] = outer.reshape(n_atom, ROWS, HALF).astype(BF16)
+            send_pair[k, :, 2 * h + 1] = inner_part.reshape(n_atom, ROWS, HALF).astype(BF16)
 
         def send(q, carry):
             to_atom(
@@ -411,9 +412,9 @@
     strength = jnp.zeros((4, ROWS, HALF), F32)
     for k in range(3):
         drain(recv_pair.at[k], pair_recv.at[k])
-        total = send_pair[k, me]
+        total = send_pair[k, me].astype(F32)
         for q in range(n_atom - 1):
-            total = total + recv_pair[k, q]
+            total = total + recv_pair[k, q].astype(F32)
         strength = strength + total * total
 
     for h in range(2):
@@ -457,8 +458,8 @@
     for q in range(n_atom - 1):
         row_sums = row_sums + recv_sum[q]
     diffusivity = prefactor * row_sums
-    diff_ref[:, :HALF] = diffusivity[0:1]
-    diff_ref[:, HALF:] = diffusivity[1:2]
+    out_ref[0:1, :HALF] = diffusivity[0:1]
+    out_ref[0:1, HALF:] = diffusivity[1:2]
     running = capacity * diffusivity
     lane_two = iota((2, HALF), 1)
     for step in (1, 2, 4, 8, 16, 32, 64):
@@ -475,8 +476,8 @@
         jnp.sum(jnp.sum(recv_total[...], axis=(0, 1)), axis=0, keepdims=True), axis=1, keepdims=True
     )
     conductivity = (earlier + running) / MODE_DEV
-    cond_ref[:, :HALF] = conductivity[0:1]
-    cond_ref[:, HALF:] = conductivity[1:2]
+    out_ref[1:2, :HALF] = conductivity[0:1]
+    out_ref[1:2, HALF:] = conductivity[1:2]
 
     up_rows.wait_send()
     down_rows.wait_send()
@@ -506,14 +507,13 @@
     any_spec = pl.BlockSpec(memory_space=pl.ANY)
     vmem_spec = pl.BlockSpec(memory_space=pltpu.VMEM)
     dma = pltpu.SemaphoreType.DMA
-    diffusivity, conductivity = pl.pallas_call(
+    (both,) = pl.pallas_call(
         functools.partial(kernel, n_atom, n_mode),
         out_shape=(
-            jax.ShapeDtypeStruct((1, MODE_DEV), F32),
-            jax.ShapeDtypeStruct((1, MODE_DEV), F32),
+            jax.ShapeDtypeStruct((2, MODE_DEV), F32),
         ),
         in_specs=[any_spec] * 6,
-        out_specs=(vmem_spec, vmem_spec),
+        out_specs=(vmem_spec,),
         scratch_shapes=[
             pltpu.VMEM((3, ATOM_DEV, MODE_DEV), BF16),
             pltpu.VMEM((3, 3, NBR, ATOM_DEV), F32),
@@ -532,8 +532,8 @@
             pltpu.VMEM((9, ATOM_DEV, 3 * RIM), BF16),
             pltpu.VMEM((3, ATOM_DEV, MODE_DEV), BF16),
             pltpu.VMEM((MODE_DEV + 2 * HALF, 3 * ATOM_DEV), BF16),
-            pltpu.VMEM((3, n_atom, 4, ROWS, HALF), F32),
-            pltpu.VMEM((3, n_atom - 1, 4, ROWS, HALF), F32),
+            pltpu.VMEM((3, n_atom, 4, ROWS, HALF), BF16),
+            pltpu.VMEM((3, n_atom - 1, 4, ROWS, HALF), BF16),
             pltpu.VMEM((MODE_DEV + 2 * HALF, HALF), F32),
             pltpu.VMEM((2, HALF), F32),
             pltpu.VMEM((n_atom - 1, 2, HALF), F32),
@@ -556,10 +556,10 @@
             pltpu.SemaphoreType.REGULAR((2,)),
         ],
         compiler_params=pltpu.CompilerParams(
-            collective_id=0, has_side_effects=True, vmem_limit_bytes=63 * 1024 * 1024
+            collective_id=0, has_side_effects=True, vmem_limit_bytes=56549376
         ),
     )(eigvec, force, bond, nbr, band, freq.reshape(1, MODE_DEV))
-    return diffusivity.reshape(MODE_DEV), conductivity.reshape(MODE_DEV)
+    return both[0], both[1]
 
 
 def solution(mesh):

time: 35.8 us -> 30.4 us (0.85)
  Pallas kernels: 33.1 us -> 28.3 us
  local copies, waits for them, and re-layouts: 1.86 us -> 1.24 us
    pallas_call x1, Pallas kernels: 33.1 us -> 28.3 us  [body(): pl.pallas_call(functools.partial(kernel, n_atom, n_mode), out_shape=(jax....]
    unnamed x6 -> x2, local copies, waits for them, and re-layouts: 1.86 us -> 0.67 us
    slice x0 -> x1, local copies, waits for them, and re-layouts: none -> 0.57 us  [body(): return (both[0], both[1])]
where the time goes in v4:
time: 30.4 us; the launch traced here: 30.2 us
  Pallas kernels  28.3 us (93%)
  local copies, waits for them, and re-layouts  1.24 us (4%)
  between operations  0.65 us (2%)
    pallas_call x1, Pallas kernels, body(): pl.pallas_call(functools.partial(kernel, n_atom, n_mode), out_shape=(jax....  28.3 us
    unnamed x2, local copies, waits for them, and re-layouts  0.67 us

profile of v4, /device:TPU:1, one launch (start us, length us, event | category | flops | bytes accessed | tf_op | source)
XLA Modules:
  0.0 30.2 jit_solution(2669189856165077342)
XLA Ops:
  0.6 0.0 copy-start
  0.6 0.7 %copy-done = f32[256]{0:T(256)S(1)} copy-done((f32[256]{0:T(256)S(1)}, f32[256]{0:T(256)}, u32[]{:S(2)}) %copy-start) | copy-done | bytes 1048
  1.3 28.3 %shard_map.77 = f32[2,256]{1,0:T(2,128)S(1)} custom-call(bf16[3,256,256]{2,1,0:T(8,128)(2,1)} %eig_hbm.1, f32[3,3,16,256]{3,2,1,0:T(8,128)} %force_hbm.1, f32[3,16,256]{2,1,0:T(8,128)} %bond_hbm.1, s32[16,256]{1,0:T(8,128)} %nbr_hbm.1, s32[2,256]{1,0:T(2,128)} %band_hbm.1, f32[1,256]{1,0:T(1,128)S(1)} %bitcast.3), custom_call_target="tpu_custom_call" | custom-call | tf_op jit(solution)/shard_map/pallas_call | solution.py:510
  29.6 0.6 %fusion = (f32[1,256]{1,0:T(1,128)}, f32[1,256]{1,0:T(1,128)}) fusion(f32[2,256]{1,0:T(2,128)S(1)} %shard_map.77), kind=kLoop, calls=%fused_computation | loop fusion | bytes 4096 | tf_op jit(solution)/shard_map/slice | solution.py:562
Async XLA Ops:
  0.6 0.7 %copy-start = (f32[256]{0:T(256)S(1)}, f32[256]{0:T(256)}, u32[]{:S(2)}) copy-start(f32[256]{0:T(256)} %param.11) | copy-start | bytes 3076

commit v5 on v4

--- a/solution.py
+++ b/solution.py
@@ -17,6 +17,7 @@
 GROUP = 16
 GROUPS = ATOM_DEV // GROUP
 ROWS = 8
+SIDE = 4
 BF16 = jnp.bfloat16
 F32 = jnp.float32
 MESH = pl.DeviceIdType.MESH
@@ -92,14 +93,20 @@
 
     barrier = pltpu.get_barrier_semaphore()
 
-    def greet_atom(q, carry):
-        pl.semaphore_signal(
-            barrier, inc=1, device_id=(lax.rem(me + q, n_atom), block), device_id_type=MESH
-        )
-        return carry
-
     recv_total[...] = jnp.zeros_like(recv_total)
-    lax.fori_loop(1, n_atom, greet_atom, 0)
+    x, y = me & (SIDE - 1), me // SIDE
+
+    def across(dx, dy):
+        return ((y + dy) & (SIDE - 1)) * SIDE + ((x + dx) & (SIDE - 1))
+
+    adjacent = (across(1, 0), across(SIDE - 1, 0), across(0, 1), across(0, SIDE - 1))
+    ring = (lax.rem(me + 1, n_atom), lax.rem(me + n_atom - 1, n_atom))
+
+    def signal(sem, atom, mode):
+        pl.semaphore_signal(sem, inc=1, device_id=(atom, mode), device_id_type=MESH)
+
+    for peer in adjacent + ring:
+        signal(barrier, peer, block)
 
     def beside(shift, action):
         @pl.when(block + shift < n_mode)
@@ -110,10 +117,7 @@
         def _():
             action(block - shift)
 
-    def greet_mode(other):
-        pl.semaphore_signal(barrier, inc=1, device_id=(me, other), device_id_type=MESH)
-
-    beside(1, greet_mode)
+    beside(1, lambda other: signal(barrier, me, other))
 
     loads = [
         pltpu.make_async_copy(nbr_hbm, nbr, local_sem.at[0]),
@@ -126,35 +130,9 @@
     for load in loads:
         load.start()
 
-    lane = iota((ATOM_DEV, 256), 1)
-    diagonal = (iota((ATOM_DEV, 256), 0) & (GROUP - 1)) == (lane & (GROUP - 1))
-    slot_rows = jnp.where(
-        (iota((NBR, 256), 1) >> 4) == iota((NBR, 256), 0), 1.0, 0.0
-    ).astype(BF16)
-
-    loads[0].wait()
-    atom_ids = iota((NBR, ATOM_DEV), 1)
-    offset = ((nbr[...] - me * ATOM_DEV - atom_ids + RIM + atoms) & (atoms - 1)) - RIM
-    column = jnp.where(offset == RIM, atom_ids, (atom_ids + offset) & (ATOM_DEV - 1))
-    nbr_cols[...] = column.astype(F32).T
-
-    col_ids = iota((GROUP, ATOM_DEV), 1).astype(F32)
-
-    def one_hot(g, carry):
-        own_cols = nbr_cols[pl.ds(pl.multiple_of(g * GROUP, GROUP), GROUP), :]
-        for n in range(NBR):
-            hot[g, n * GROUP : (n + 1) * GROUP, :] = jnp.where(
-                own_cols[:, n : n + 1] == col_ids, 1.0, 0.0
-            ).astype(BF16)
-        return carry
-
-    lax.fori_loop(0, GROUPS, one_hot, 0, unroll=4)
-
-    loads[5].wait()
-    loads[3].wait()
     pl.semaphore_wait(
         barrier,
-        n_atom - 1 + (block > 0).astype(jnp.int32) + (block < n_mode - 1).astype(jnp.int32),
+        6 + (block > 0).astype(jnp.int32) + (block < n_mode - 1).astype(jnp.int32),
     )
 
     def to_atom(src, dst, q, send, recv):
@@ -178,16 +156,16 @@
         )
 
     up_rows = to_atom(
-        eig.at[:, pl.ds(ATOM_DEV - RIM, RIM), :], low_rows, 1, row_send.at[0], row_recv.at[0]
+        eig_hbm.at[:, pl.ds(ATOM_DEV - RIM, RIM), :], low_rows, 1, row_send.at[0], row_recv.at[0]
     )
     down_rows = to_atom(
-        eig.at[:, pl.ds(0, RIM), :], high_rows, n_atom - 1, row_send.at[1], row_recv.at[1]
+        eig_hbm.at[:, pl.ds(0, RIM), :], high_rows, n_atom - 1, row_send.at[1], row_recv.at[1]
     )
     up_cols = to_mode(
-        eig.at[:, :, pl.ds(MODE_DEV - HALF, HALF)], low_cols, 1, col_send.at[0], col_recv.at[0]
+        eig_hbm.at[:, :, pl.ds(MODE_DEV - HALF, HALF)], low_cols, 1, col_send.at[0], col_recv.at[0]
     )
     down_cols = to_mode(
-        eig.at[:, :, pl.ds(0, HALF)], high_cols, n_mode - 1, col_send.at[1], col_recv.at[1]
+        eig_hbm.at[:, :, pl.ds(0, HALF)], high_cols, n_mode - 1, col_send.at[1], col_recv.at[1]
     )
     up_rows.start()
     down_rows.start()
@@ -200,21 +178,8 @@
     def _():
         down_cols.start()
 
-    @pl.when(block > 0)
-    def _():
-        pl.semaphore_wait(ready.at[0], 1)
-
-    @pl.when(block < n_mode - 1)
-    def _():
-        pl.semaphore_signal(
-            ready.at[0], inc=1, device_id=(me, block + 1), device_id_type=MESH
-        )
-
-    def tell(other, carry):
-        pl.semaphore_signal(ready.at[1], inc=1, device_id=(me, other), device_id_type=MESH)
-        return carry
-
-    lax.fori_loop(0, block, tell, 0)
+    for peer in adjacent:
+        signal(ready.at[2], peer, block)
 
     def send_freq(q, carry):
         to_mode(
@@ -226,8 +191,58 @@
         ).start()
         return carry
 
+
+    lane = iota((ATOM_DEV, 256), 1)
+    diagonal = (iota((ATOM_DEV, 256), 0) & (GROUP - 1)) == (lane & (GROUP - 1))
+    slot_rows = jnp.where(
+        (iota((NBR, 256), 1) >> 4) == iota((NBR, 256), 0), 1.0, 0.0
+    ).astype(BF16)
+
+    loads[0].wait()
+    atom_ids = iota((NBR, ATOM_DEV), 1)
+    offset = ((nbr[...] - me * ATOM_DEV - atom_ids + RIM + atoms) & (atoms - 1)) - RIM
+    column = jnp.where(offset == RIM, atom_ids, (atom_ids + offset) & (ATOM_DEV - 1))
+    nbr_cols[...] = column.astype(F32).T
+
+    col_ids = iota((GROUP, ATOM_DEV), 1).astype(F32)
+
+    def one_hot(g, carry):
+        own_cols = nbr_cols[pl.ds(pl.multiple_of(g * GROUP, GROUP), GROUP), :]
+        for n in range(NBR):
+            hot[g, n * GROUP : (n + 1) * GROUP, :] = jnp.where(
+                own_cols[:, n : n + 1] == col_ids, 1.0, 0.0
+            ).astype(BF16)
+        return carry
+
+    lax.fori_loop(0, GROUPS, one_hot, 0, unroll=4)
+
+    pl.semaphore_wait(ready.at[2], len(adjacent))
+    signal(ready.at[3], across(2, 0), block)
+    signal(ready.at[3], across(0, 2), block)
+    loads[5].wait()
+
+    @pl.when(block > 0)
+    def _():
+        pl.semaphore_wait(ready.at[0], 1)
+
+    @pl.when(block < n_mode - 1)
+    def _():
+        signal(ready.at[0], me, block + 1)
+
+    def tell(sem):
+        def one(other, carry):
+            signal(sem, me, other)
+            return carry
+
+        lax.fori_loop(0, block, one, 0)
+
+    def hear(sem):
+        @pl.when(block < n_mode - 1)
+        def _():
+            pl.semaphore_wait(sem, n_mode - 1 - block)
+
+    tell(ready.at[4])
     lax.fori_loop(n_mode - block, n_mode, send_freq, 0)
-
     loads[1].wait()
     loads[2].wait()
 
@@ -324,6 +339,7 @@
 
     spread_out()
     build()
+    loads[3].wait()
     for k in range(3):
         inner_part_of(k)
     for c in range(3):
@@ -350,13 +366,11 @@
         eig_t[HALF + MODE_DEV :, c * ATOM_DEV : (c + 1) * ATOM_DEV] = high_cols[c].T
     up_rows.wait_recv()
     down_rows.wait_recv()
+    pl.semaphore_wait(ready.at[3], 2)
+    tell(ready.at[1])
     project(0)
     project(1)
-
-    @pl.when(block < n_mode - 1)
-    def _():
-        pl.semaphore_wait(ready.at[1], n_mode - 1 - block)
-
+    hear(ready.at[4])
     lax.fori_loop(1, n_mode - block, send_freq, 0)
     project(2)
 
@@ -452,6 +466,7 @@
 
         return lax.fori_loop(0, n_atom, share_to, carry, unroll=True)
 
+    hear(ready.at[1])
     lax.fori_loop(0, n_mode - 1 - block, share_total, 0)
     drain(recv_sum, sum_recv)
     row_sums = send_sum[...]
@@ -553,7 +568,7 @@
             dma(()),
             dma((n_mode - 1,)),
             dma((n_mode - 1,)),
-            pltpu.SemaphoreType.REGULAR((2,)),
+            pltpu.SemaphoreType.REGULAR((5,)),
         ],
         compiler_params=pltpu.CompilerParams(
             collective_id=0, has_side_effects=True, vmem_limit_bytes=56549376

time: 30.4 us -> 29.7 us (0.977)
  Pallas kernels: 28.3 us -> 27.7 us
    pallas_call x1, Pallas kernels: 28.3 us -> 27.7 us  [body(): pl.pallas_call(functools.partial(kernel, n_atom, n_mode), out_shape=(jax....]
where the time goes in v5:
time: 29.7 us; the launch traced here: 29.6 us
  Pallas kernels  27.7 us (93%)
  local copies, waits for them, and re-layouts  1.24 us (4%)
  between operations  0.65 us (2%)
    pallas_call x1, Pallas kernels, body(): pl.pallas_call(functools.partial(kernel, n_atom, n_mode), out_shape=(jax....  27.7 us
    unnamed x2, local copies, waits for them, and re-layouts  0.67 us

profile of v5, /device:TPU:1, one launch (start us, length us, event | category | flops | bytes accessed | tf_op | source)
XLA Modules:
  0.0 29.6 jit_solution(7584065321226145389)
XLA Ops:
  0.6 0.0 copy-start
  0.6 0.7 %copy-done = f32[256]{0:T(256)S(1)} copy-done((f32[256]{0:T(256)S(1)}, f32[256]{0:T(256)}, u32[]{:S(2)}) %copy-start) | copy-done | bytes 1048
  1.3 27.7 %shard_map.77 = f32[2,256]{1,0:T(2,128)S(1)} custom-call(bf16[3,256,256]{2,1,0:T(8,128)(2,1)} %eig_hbm.1, f32[3,3,16,256]{3,2,1,0:T(8,128)} %force_hbm.1, f32[3,16,256]{2,1,0:T(8,128)} %bond_hbm.1, s32[16,256]{1,0:T(8,128)} %nbr_hbm.1, s32[2,256]{1,0:T(2,128)} %band_hbm.1, f32[1,256]{1,0:T(1,128)S(1)} %bitcast.3), custom_call_target="tpu_custom_call" | custom-call | tf_op jit(solution)/shard_map/pallas_call | solution.py:525
  29.0 0.6 %fusion = (f32[1,256]{1,0:T(1,128)}, f32[1,256]{1,0:T(1,128)}) fusion(f32[2,256]{1,0:T(2,128)S(1)} %shard_map.77), kind=kLoop, calls=%fused_computation | loop fusion | bytes 4096 | tf_op jit(solution)/shard_map/slice | solution.py:577
Async XLA Ops:
  0.6 0.7 %copy-start = (f32[256]{0:T(256)S(1)}, f32[256]{0:T(256)}, u32[]{:S(2)}) copy-start(f32[256]{0:T(256)} %param.11) | copy-start | bytes 3076

commit v6 on v5

--- a/solution.py
+++ b/solution.py
@@ -18,6 +18,10 @@
 GROUPS = ATOM_DEV // GROUP
 ROWS = 8
 SIDE = 4
+FAR_FIRST = sorted(
+    ((dx, dy) for dx in range(SIDE) for dy in range(SIDE) if dx or dy),
+    key=lambda step: -sum(min(part, SIDE - part) for part in step),
+)
 BF16 = jnp.bfloat16
 F32 = jnp.float32
 MESH = pl.DeviceIdType.MESH
@@ -155,20 +159,33 @@
             device_id_type=MESH,
         )
 
-    up_rows = to_atom(
-        eig_hbm.at[:, pl.ds(ATOM_DEV - RIM, RIM), :], low_rows, 1, row_send.at[0], row_recv.at[0]
-    )
-    down_rows = to_atom(
-        eig_hbm.at[:, pl.ds(0, RIM), :], high_rows, n_atom - 1, row_send.at[1], row_recv.at[1]
-    )
+    def rim_copies(h):
+        cols = pl.ds(h * HALF, HALF)
+        up = to_atom(
+            eig_hbm.at[:, pl.ds(ATOM_DEV - RIM, RIM), cols],
+            low_rows.at[h],
+            1,
+            row_send.at[h, 0],
+            row_recv.at[h, 0],
+        )
+        down = to_atom(
+            eig_hbm.at[:, pl.ds(0, RIM), cols],
+            high_rows.at[h],
+            n_atom - 1,
+            row_send.at[h, 1],
+            row_recv.at[h, 1],
+        )
+        return up, down
+
+    rims = rim_copies(0) + rim_copies(1)
     up_cols = to_mode(
         eig_hbm.at[:, :, pl.ds(MODE_DEV - HALF, HALF)], low_cols, 1, col_send.at[0], col_recv.at[0]
     )
     down_cols = to_mode(
         eig_hbm.at[:, :, pl.ds(0, HALF)], high_cols, n_mode - 1, col_send.at[1], col_recv.at[1]
     )
-    up_rows.start()
-    down_rows.start()
+    for rim in rims:
+        rim.start()
 
     @pl.when(block < n_mode - 1)
     def _():
@@ -303,39 +320,37 @@
             0,
         ).reshape(3, ATOM_DEV, MODE_DEV)
 
-    def project(k):
-        for h, halo in enumerate((low_rows, high_rows)):
+    def project(h, k):
+        ours = slice(h * HALF, (h + 1) * HALF)
+        for side, halo in enumerate((low_rows, high_rows)):
+            rows = slice(side * RIM, (side + 1) * RIM)
             outer = contract(
-                rim_m[3 * k : 3 * k + 3, h * RIM : (h + 1) * RIM, :].reshape(3 * RIM, 3 * RIM),
-                halo[...].reshape(3 * RIM, MODE_DEV),
+                rim_m[3 * k : 3 * k + 3, rows, :].reshape(3 * RIM, 3 * RIM),
+                halo[h].reshape(3 * RIM, HALF),
                 1,
                 0,
-            ).reshape(3, RIM, MODE_DEV)
-            flux[:, h * RIM : (h + 1) * RIM, :] = (
-                inner_flux[3 * k : 3 * k + 3, h * RIM : (h + 1) * RIM, :] + outer
-            ).astype(BF16)
-        pair = contract(eig_t[...], flux[...].reshape(3 * ATOM_DEV, MODE_DEV), 1, 0)
-        for h in range(2):
-            ours = slice(h * HALF, (h + 1) * HALF)
-            before = pair[h * HALF : (h + 1) * HALF, ours]
-            level = pair[(h + 1) * HALF : (h + 2) * HALF, ours]
-            after = pair[(h + 2) * HALF : (h + 3) * HALF, ours]
-            outer = jnp.where(row > col, before, after)
-            inner_part = jnp.where(row == col, before, level)
-            send_pair[k, :, 2 * h] = outer.reshape(n_atom, ROWS, HALF).astype(BF16)
-            send_pair[k, :, 2 * h + 1] = inner_part.reshape(n_atom, ROWS, HALF).astype(BF16)
-
-        def send(q, carry):
-            to_atom(
-                send_pair.at[k, lax.rem(me + q, n_atom)],
-                recv_pair.at[k, q - 1],
-                q,
-                pair_send.at[k],
-                pair_recv.at[k],
+            ).reshape(3, RIM, HALF)
+            flux[h, :, rows, :] = (inner_flux[3 * k : 3 * k + 3, rows, ours] + outer).astype(BF16)
+        pair = contract(
+            eig_t[h * HALF : (h + 3) * HALF], flux[h].reshape(3 * ATOM_DEV, HALF), 1, 0
+        )
+        before, level, after = (pair[s * HALF : (s + 1) * HALF] for s in range(3))
+        outer = jnp.where(row > col, before, after)
+        inner_part = jnp.where(row == col, before, level)
+        send_pair[h, :, k, 0] = outer.reshape(n_atom, ROWS, HALF).astype(BF16)
+        send_pair[h, :, k, 1] = inner_part.reshape(n_atom, ROWS, HALF).astype(BF16)
+
+    def scatter(h):
+        for slot, (dx, dy) in enumerate(FAR_FIRST):
+            peer = across(dx, dy)
+            pltpu.make_async_remote_copy(
+                src_ref=send_pair.at[h, peer],
+                dst_ref=recv_pair.at[h, slot],
+                send_sem=pair_send.at[h],
+                recv_sem=pair_recv.at[h],
+                device_id=(peer, block),
+                device_id_type=MESH,
             ).start()
-            return carry
-
-        lax.fori_loop(1, n_atom, send, 0)
 
     spread_out()
     build()
@@ -364,15 +379,20 @@
     for c in range(3):
         eig_t[:HALF, c * ATOM_DEV : (c + 1) * ATOM_DEV] = low_cols[c].T
         eig_t[HALF + MODE_DEV :, c * ATOM_DEV : (c + 1) * ATOM_DEV] = high_cols[c].T
-    up_rows.wait_recv()
-    down_rows.wait_recv()
+    for rim in rims[:2]:
+        rim.wait_recv()
     pl.semaphore_wait(ready.at[3], 2)
     tell(ready.at[1])
-    project(0)
-    project(1)
+    for k in range(3):
+        project(0, k)
+    scatter(0)
+    for rim in rims[2:]:
+        rim.wait_recv()
+    for k in range(3):
+        project(1, k)
+    scatter(1)
     hear(ready.at[4])
     lax.fori_loop(1, n_mode - block, send_freq, 0)
-    project(2)
 
     loads[4].wait()
     drain(spectrum.at[pl.ds(1, n_mode - 1), :], freq_recv)
@@ -423,26 +443,27 @@
             factor = (mine + partner) ** 2 / (4.0 * mine * partner)
             weights.append((inside, lorentz * factor))
 
-    strength = jnp.zeros((4, ROWS, HALF), F32)
-    for k in range(3):
-        drain(recv_pair.at[k], pair_recv.at[k])
-        total = send_pair[k, me].astype(F32)
+    for h in range(2):
+        drain(recv_pair.at[h], pair_recv.at[h])
+        total = send_pair[h, me].astype(F32)
         for q in range(n_atom - 1):
-            total = total + recv_pair[k, q].astype(F32)
-        strength = strength + total * total
-
-    for h in range(2):
+            total = total + recv_pair[h, q].astype(F32)
+        strength = jnp.sum(total * total, axis=0)
         term = 0.0
         for s in range(2):
             inside, weight = weights[2 * h + s]
-            term = term + jnp.where(inside, weight * strength[2 * h + s], 0.0)
+            term = term + jnp.where(inside, weight * strength[s], 0.0)
         send_sum[h : h + 1] = jnp.sum(term, axis=0, keepdims=True)
 
-    def share(q, carry):
-        to_atom(send_sum, recv_sum.at[q - 1], q, sum_send, sum_recv).start()
-        return carry
-
-    lax.fori_loop(1, n_atom, share, 0)
+    for slot, (dx, dy) in enumerate(FAR_FIRST):
+        pltpu.make_async_remote_copy(
+            src_ref=send_sum,
+            dst_ref=recv_sum.at[slot],
+            send_sem=sum_send,
+            recv_sem=sum_recv,
+            device_id=(across(dx, dy), block),
+            device_id_type=MESH,
+        ).start()
     freq_two = jnp.concatenate([own_freq[:, :HALF], own_freq[:, HALF:]], axis=0)
     grown = jnp.exp(freq_two)
     capacity = freq_two * freq_two * grown / ((grown - 1.0) * (grown - 1.0))
@@ -450,24 +471,20 @@
     part_total = capacity * prefactor * send_sum[...]
     send_total[...] = part_total[0:1] + part_total[1:2]
 
-    def share_total(t, carry):
-        shift = n_mode - 1 - block - t
-
-        def share_to(q, carry):
+    def share_total(shift):
+        for slot, (dx, dy) in enumerate(FAR_FIRST + [(0, 0)]):
             pltpu.make_async_remote_copy(
                 src_ref=send_total,
-                dst_ref=recv_total.at[shift - 1, q],
+                dst_ref=recv_total.at[shift - 1, slot],
                 send_sem=total_send.at[shift - 1],
                 recv_sem=total_recv.at[shift - 1],
-                device_id=(lax.rem(me + q, n_atom), block + shift),
+                device_id=(across(dx, dy), block + shift),
                 device_id_type=MESH,
             ).start()
-            return carry
-
-        return lax.fori_loop(0, n_atom, share_to, carry, unroll=True)
 
     hear(ready.at[1])
-    lax.fori_loop(0, n_mode - 1 - block, share_total, 0)
+    for shift in range(n_mode - 1, 0, -1):
+        pl.when(block + shift < n_mode)(functools.partial(share_total, shift))
     drain(recv_sum, sum_recv)
     row_sums = send_sum[...]
     for q in range(n_atom - 1):
@@ -494,8 +511,8 @@
     out_ref[1:2, :HALF] = conductivity[0:1]
     out_ref[1:2, HALF:] = conductivity[1:2]
 
-    up_rows.wait_send()
-    down_rows.wait_send()
+    for rim in rims:
+        rim.wait_send()
 
     @pl.when(block < n_mode - 1)
     def _():
@@ -506,8 +523,8 @@
         down_cols.wait_send()
 
     drain(spectrum.at[pl.ds(1, n_mode - 1), :], freq_send)
-    for k in range(3):
-        drain(recv_pair.at[k], pair_send.at[k])
+    for h in range(2):
+        drain(recv_pair.at[h], pair_send.at[h])
     drain(recv_sum, sum_send)
 
     def sent_total(t, carry):
@@ -519,6 +536,7 @@
 
 def body(eigvec, force, bond, nbr, band, freq):
     n_atom, n_mode = lax.axis_size("atom"), lax.axis_size("mode")
+    operands = (eigvec, force, bond, nbr, band, freq.reshape(1, MODE_DEV))
     any_spec = pl.BlockSpec(memory_space=pl.ANY)
     vmem_spec = pl.BlockSpec(memory_space=pltpu.VMEM)
     dma = pltpu.SemaphoreType.DMA
@@ -536,8 +554,8 @@
             pltpu.VMEM((NBR, ATOM_DEV), jnp.int32),
             pltpu.VMEM((2, MODE_DEV), jnp.int32),
             pltpu.VMEM((n_mode, MODE_DEV), F32),
-            pltpu.VMEM((3, RIM, MODE_DEV), BF16),
-            pltpu.VMEM((3, RIM, MODE_DEV), BF16),
+            pltpu.VMEM((2, 3, RIM, HALF), BF16),
+            pltpu.VMEM((2, 3, RIM, HALF), BF16),
             pltpu.VMEM((3, ATOM_DEV, HALF), BF16),
             pltpu.VMEM((3, ATOM_DEV, HALF), BF16),
             pltpu.VMEM((ATOM_DEV, NBR), F32),
@@ -545,10 +563,10 @@
             pltpu.VMEM((GROUPS, 27 * GROUP, 256), BF16),
             pltpu.VMEM((9, ATOM_DEV, 3 * ATOM_DEV), BF16),
             pltpu.VMEM((9, ATOM_DEV, 3 * RIM), BF16),
-            pltpu.VMEM((3, ATOM_DEV, MODE_DEV), BF16),
+            pltpu.VMEM((2, 3, ATOM_DEV, HALF), BF16),
             pltpu.VMEM((MODE_DEV + 2 * HALF, 3 * ATOM_DEV), BF16),
-            pltpu.VMEM((3, n_atom, 4, ROWS, HALF), BF16),
-            pltpu.VMEM((3, n_atom - 1, 4, ROWS, HALF), BF16),
+            pltpu.VMEM((2, n_atom, 3, 2, ROWS, HALF), BF16),
+            pltpu.VMEM((2, n_atom - 1, 3, 2, ROWS, HALF), BF16),
             pltpu.VMEM((MODE_DEV + 2 * HALF, HALF), F32),
             pltpu.VMEM((2, HALF), F32),
             pltpu.VMEM((n_atom - 1, 2, HALF), F32),
@@ -556,14 +574,14 @@
             pltpu.VMEM((n_mode - 1, n_atom, 1, HALF), F32),
             pltpu.VMEM((9, ATOM_DEV, MODE_DEV), F32),
             dma((6,)),
-            dma((2,)),
-            dma((2,)),
+            dma((2, 2)),
+            dma((2, 2)),
             dma((2,)),
             dma((2,)),
             dma(()),
             dma(()),
-            dma((3,)),
-            dma((3,)),
+            dma((2,)),
+            dma((2,)),
             dma(()),
             dma(()),
             dma((n_mode - 1,)),
@@ -571,9 +589,9 @@
             pltpu.SemaphoreType.REGULAR((5,)),
         ],
         compiler_params=pltpu.CompilerParams(
-            collective_id=0, has_side_effects=True, vmem_limit_bytes=56549376
+            collective_id=0, has_side_effects=True, vmem_limit_bytes=40 * 1024 * 1024
         ),
-    )(eigvec, force, bond, nbr, band, freq.reshape(1, MODE_DEV))
+    )(*(pltpu.with_memory_space_constraint(part, pltpu.HBM) for part in operands))
     return both[0], both[1]
 
 

time: 29.7 us -> 28.4 us (0.956)
  Pallas kernels: 27.7 us -> 26.9 us
  local copies, waits for them, and re-layouts: 1.24 us -> 0.57 us
    pallas_call x1, Pallas kernels: 27.7 us -> 26.9 us  [body(): pl.pallas_call(functools.partial(kernel, n_atom, n_mode), out_shape=(jax....]
    unnamed x2 -> x0, local copies, waits for them, and re-layouts: 0.67 us -> none
where the time goes in v6:
time: 28.4 us; the launch traced here: 28.1 us
  Pallas kernels  26.9 us (95%)
  between operations  0.64 us (2%)
  local copies, waits for them, and re-layouts  0.57 us (2%)
    pallas_call x1, Pallas kernels, body(): pl.pallas_call(functools.partial(kernel, n_atom, n_mode), out_shape=(jax....  26.9 us
    slice x1, local copies, waits for them, and re-layouts, body(): return (both[0], both[1])  0.57 us

profile of v6, /device:TPU:1, one launch (start us, length us, event | category | flops | bytes accessed | tf_op | source)
XLA Modules:
  0.0 28.1 jit_solution(8334794828155717997)
XLA Ops:
  0.6 26.9 %shard_map.77 = f32[2,256]{1,0:T(2,128)S(1)} custom-call(bf16[3,256,256]{2,1,0:T(8,128)(2,1)} %eig_hbm.1, f32[3,3,16,256]{3,2,1,0:T(8,128)} %force_hbm.1, f32[3,16,256]{2,1,0:T(8,128)} %bond_hbm.1, s32[16,256]{1,0:T(8,128)} %nbr_hbm.1, s32[2,256]{1,0:T(2,128)} %band_hbm.1, f32[1,256]{1,0:T(1,128)} %bitcast.3), custom_call_target="tpu_custom_call" | custom-call | tf_op jit(solution)/shard_map/pallas_call | solution.py:543
  27.6 0.6 %fusion = (f32[1,256]{1,0:T(1,128)}, f32[1,256]{1,0:T(1,128)}) fusion(f32[2,256]{1,0:T(2,128)S(1)} %shard_map.77), kind=kLoop, calls=%fused_computation | loop fusion | bytes 4096 | tf_op jit(solution)/shard_map/slice | solution.py:595

commit v7 on v6

--- a/solution.py
+++ b/solution.py
@@ -104,6 +104,7 @@
         return ((y + dy) & (SIDE - 1)) * SIDE + ((x + dx) & (SIDE - 1))
 
     adjacent = (across(1, 0), across(SIDE - 1, 0), across(0, 1), across(0, SIDE - 1))
+    peers = [across(dx, dy) for dx, dy in FAR_FIRST]
     ring = (lax.rem(me + 1, n_atom), lax.rem(me + n_atom - 1, n_atom))
 
     def signal(sem, atom, mode):
@@ -133,6 +134,18 @@
     ]
     for load in loads:
         load.start()
+
+    lane = iota((ATOM_DEV, 256), 1)
+    diagonal = (iota((ATOM_DEV, 256), 0) & (GROUP - 1)) == (lane & (GROUP - 1))
+    slot_rows = jnp.where(
+        (iota((NBR, 256), 1) >> 4) == iota((NBR, 256), 0), 1.0, 0.0
+    ).astype(BF16)
+
+    loads[0].wait()
+    atom_ids = iota((NBR, ATOM_DEV), 1)
+    offset = ((nbr[...] - me * ATOM_DEV - atom_ids + RIM + atoms) & (atoms - 1)) - RIM
+    column = jnp.where(offset == RIM, atom_ids, (atom_ids + offset) & (ATOM_DEV - 1))
+    nbr_cols[...] = column.astype(F32).T
 
     pl.semaphore_wait(
         barrier,
@@ -209,18 +222,6 @@
         return carry
 
 
-    lane = iota((ATOM_DEV, 256), 1)
-    diagonal = (iota((ATOM_DEV, 256), 0) & (GROUP - 1)) == (lane & (GROUP - 1))
-    slot_rows = jnp.where(
-        (iota((NBR, 256), 1) >> 4) == iota((NBR, 256), 0), 1.0, 0.0
-    ).astype(BF16)
-
-    loads[0].wait()
-    atom_ids = iota((NBR, ATOM_DEV), 1)
-    offset = ((nbr[...] - me * ATOM_DEV - atom_ids + RIM + atoms) & (atoms - 1)) - RIM
-    column = jnp.where(offset == RIM, atom_ids, (atom_ids + offset) & (ATOM_DEV - 1))
-    nbr_cols[...] = column.astype(F32).T
-
     col_ids = iota((GROUP, ATOM_DEV), 1).astype(F32)
 
     def one_hot(g, carry):
@@ -231,11 +232,8 @@
             ).astype(BF16)
         return carry
 
-    lax.fori_loop(0, GROUPS, one_hot, 0, unroll=4)
-
-    pl.semaphore_wait(ready.at[2], len(adjacent))
-    signal(ready.at[3], across(2, 0), block)
-    signal(ready.at[3], across(0, 2), block)
+    lax.fori_loop(0, GROUPS, one_hot, 0, unroll=8)
+
     loads[5].wait()
 
     @pl.when(block > 0)
@@ -341,8 +339,7 @@
         send_pair[h, :, k, 1] = inner_part.reshape(n_atom, ROWS, HALF).astype(BF16)
 
     def scatter(h):
-        for slot, (dx, dy) in enumerate(FAR_FIRST):
-            peer = across(dx, dy)
+        for slot, peer in enumerate(peers):
             pltpu.make_async_remote_copy(
                 src_ref=send_pair.at[h, peer],
                 dst_ref=recv_pair.at[h, slot],
@@ -353,6 +350,9 @@
             ).start()
 
     spread_out()
+    pl.semaphore_wait(ready.at[2], len(adjacent))
+    signal(ready.at[3], across(2, 0), block)
+    signal(ready.at[3], across(0, 2), block)
     build()
     loads[3].wait()
     for k in range(3):
@@ -381,11 +381,11 @@
         eig_t[HALF + MODE_DEV :, c * ATOM_DEV : (c + 1) * ATOM_DEV] = high_cols[c].T
     for rim in rims[:2]:
         rim.wait_recv()
-    pl.semaphore_wait(ready.at[3], 2)
-    tell(ready.at[1])
     for k in range(3):
         project(0, k)
+    pl.semaphore_wait(ready.at[3], 2)
     scatter(0)
+    tell(ready.at[1])
     for rim in rims[2:]:
         rim.wait_recv()
     for k in range(3):
@@ -455,13 +455,13 @@
             term = term + jnp.where(inside, weight * strength[s], 0.0)
         send_sum[h : h + 1] = jnp.sum(term, axis=0, keepdims=True)
 
-    for slot, (dx, dy) in enumerate(FAR_FIRST):
+    for slot, peer in enumerate(peers):
         pltpu.make_async_remote_copy(
             src_ref=send_sum,
             dst_ref=recv_sum.at[slot],
             send_sem=sum_send,
             recv_sem=sum_recv,
-            device_id=(across(dx, dy), block),
+            device_id=(peer, block),
             device_id_type=MESH,
         ).start()
     freq_two = jnp.concatenate([own_freq[:, :HALF], own_freq[:, HALF:]], axis=0)
@@ -472,13 +472,13 @@
     send_total[...] = part_total[0:1] + part_total[1:2]
 
     def share_total(shift):
-        for slot, (dx, dy) in enumerate(FAR_FIRST + [(0, 0)]):
+        for slot, peer in enumerate(peers + [me]):
             pltpu.make_async_remote_copy(
                 src_ref=send_total,
-                dst_ref=recv_total.at[shift - 1, slot],
+                dst_ref=recv_total.at[shift - 1, pl.ds(slot, 1), :],
                 send_sem=total_send.at[shift - 1],
                 recv_sem=total_recv.at[shift - 1],
-                device_id=(across(dx, dy), block + shift),
+                device_id=(peer, block + shift),
                 device_id_type=MESH,
             ).start()
 
@@ -505,7 +505,7 @@
 
     lax.fori_loop(0, block, hear_total, 0)
     earlier = jnp.sum(
-        jnp.sum(jnp.sum(recv_total[...], axis=(0, 1)), axis=0, keepdims=True), axis=1, keepdims=True
+        jnp.sum(jnp.sum(recv_total[...], axis=0), axis=0, keepdims=True), axis=1, keepdims=True
     )
     conductivity = (earlier + running) / MODE_DEV
     out_ref[1:2, :HALF] = conductivity[0:1]
@@ -571,7 +571,7 @@
             pltpu.VMEM((2, HALF), F32),
             pltpu.VMEM((n_atom - 1, 2, HALF), F32),
             pltpu.VMEM((1, HALF), F32),
-            pltpu.VMEM((n_mode - 1, n_atom, 1, HALF), F32),
+            pltpu.VMEM((n_mode - 1, n_atom, HALF), F32),
             pltpu.VMEM((9, ATOM_DEV, MODE_DEV), F32),
             dma((6,)),
             dma((2, 2)),

time: 28.4 us -> 27.7 us (0.975)
  Pallas kernels: 26.9 us -> 26.3 us
    pallas_call x1, Pallas kernels: 26.9 us -> 26.3 us  [body(): pl.pallas_call(functools.partial(kernel, n_atom, n_mode), out_shape=(jax....]
where the time goes in v7:
time: 27.7 us; the launch traced here: 27.5 us
  Pallas kernels  26.3 us (95%)
  between operations  0.64 us (2%)
  local copies, waits for them, and re-layouts  0.57 us (2%)
    pallas_call x1, Pallas kernels, body(): pl.pallas_call(functools.partial(kernel, n_atom, n_mode), out_shape=(jax....  26.3 us
    slice x1, local copies, waits for them, and re-layouts, body(): return (both[0], both[1])  0.57 us

profile of v7, /device:TPU:1, one launch (start us, length us, event | category | flops | bytes accessed | tf_op | source)
XLA Modules:
  0.0 27.5 jit_solution(6672043222467637797)
XLA Ops:
  0.6 26.3 %shard_map.77 = f32[2,256]{1,0:T(2,128)S(1)} custom-call(bf16[3,256,256]{2,1,0:T(8,128)(2,1)} %eig_hbm.1, f32[3,3,16,256]{3,2,1,0:T(8,128)} %force_hbm.1, f32[3,16,256]{2,1,0:T(8,128)} %bond_hbm.1, s32[16,256]{1,0:T(8,128)} %nbr_hbm.1, s32[2,256]{1,0:T(2,128)} %band_hbm.1, f32[1,256]{1,0:T(1,128)} %bitcast.3), custom_call_target="tpu_custom_call" | custom-call | tf_op jit(solution)/shard_map/pallas_call | solution.py:543
  26.9 0.6 %fusion = (f32[1,256]{1,0:T(1,128)}, f32[1,256]{1,0:T(1,128)}) fusion(f32[2,256]{1,0:T(2,128)S(1)} %shard_map.77), kind=kLoop, calls=%fused_computation | loop fusion | bytes 4096 | tf_op jit(solution)/shard_map/slice | solution.py:595
